TPU v7x, 32 devices: a whole 2x2x4 slice. The times are simulated.
32 devices in a mesh: dp: 8 (over z, x), section: 4 (over y, core).
Axes of the slice: x: 2, y: 2, z: 4, core: 2. Of those that a mesh axis runs over, the one named last changes fastest.
Arguments:
- patches: bfloat16 [256, 1600], P(('dp', 'section')), may hold values from -6 to 6
- gain: float32 [1600], replicated, may hold values from 0.5 to 2
- expand_weight: bfloat16 [1600, 8192], P('dp', 'section'), may hold values from -0.15625 to 0.15625
- project_weight: bfloat16 [8192, 1600], P('section', 'dp'), may hold values from -0.0625 to 0.0625
- counts: int32 [8, 4], P('dp'), may hold values from 1 to 8
- positions: int32 [32, 8], P(('dp', 'section')), may hold values from 0 to 15, as said below
- text: bfloat16 [512, 1600], P(('dp', 'section')), may hold values from -6 to 6
- cotangent: bfloat16 [512, 1600], P(('dp', 'section')), may hold values from -6 to 6
Outputs:
- embedded: bfloat16 [512, 1600], P(('dp', 'section'))
- grad_rows: bfloat16 [256, 1600], P(('dp', 'section'))
- expand_grad: bfloat16 [1600, 8192], P(None, 'section')
- project_grad: bfloat16 [8192, 1600], P('section')
Inputs may be any that keep to these rules, and one draw needn't show every extreme that they name: `positions`: within each row the values are distinct.
All inputs are finite; a program needn't handle non-finite values.
Results may differ from a plain program's by a relative error of at most 0.015.
Values may be sent and summed in bfloat16 or wider, within the bound.
No kernel may reach another device: no remote copies, remote signals or barrier semaphores. Data moves between devices by JAX's collectives and lax.ppermute only.
A program may use at most 64 MiB of HBM per device.

v0:
```python
import jax
import jax.numpy as jnp
from jax import lax
from jax.sharding import PartitionSpec as P


def gelu_pair(values):
    coeff = 0.7978845608
    inner = coeff * (values + 0.044715 * values * values * values)
    tangent = jnp.tanh(inner)
    activated = 0.5 * values * (1.0 + tangent)
    derivative = 0.5 * (1.0 + tangent) + 0.5 * values * (1.0 - tangent * tangent) * coeff * (
        1.0 + 3.0 * 0.044715 * values * values
    )
    return (activated, derivative)


def shards(patches, gain, expand_weight, project_weight, counts, positions, text, cotangent):
    sections = lax.axis_size("section")
    slot_count = patches.shape[0]
    features = patches.shape[1]
    capacity = slot_count // sections
    inputs = patches.astype(jnp.float32)
    inv_rms = lax.rsqrt(jnp.mean(inputs * inputs, axis=-1, keepdims=True) + 1e-06)
    normed = (inputs * inv_rms * gain).astype(jnp.bfloat16)
    gathered = lax.all_gather(normed, "section", axis=0, tiled=True)
    expand_full, project_full = (
        lax.all_gather(expand_weight, "dp", axis=0, tiled=True),
        lax.all_gather(project_weight, "dp", axis=1, tiled=True),
    )
    preact = jnp.dot(gathered, expand_full, preferred_element_type=jnp.float32)
    activated, derivative = gelu_pair(preact)
    hidden = activated.astype(jnp.bfloat16)
    row_block = hidden
    mixed = lax.psum_scatter(
        jnp.dot(row_block, project_full, preferred_element_type=jnp.float32).astype(jnp.bfloat16),
        "section",
        scatter_dimension=0,
        tiled=True,
    ).astype(jnp.float32)
    out_rows = (inputs + mixed).astype(jnp.bfloat16)
    arrived = lax.all_to_all(out_rows, "section", split_axis=0, concat_axis=0, tiled=True)
    section_id = lax.axis_index("section")
    arrival = jnp.arange(slot_count, dtype=jnp.int32)
    source = arrival // capacity
    slot_index = section_id * capacity + arrival % capacity
    is_live = (slot_index < counts[0][source])[:, None]
    targets = positions[0]
    current = text[targets]
    embedded = text.at[targets].set(jnp.where(is_live, arrived, current))
    picked = jnp.where(is_live, cotangent[targets], jnp.zeros_like(current))
    collected = lax.all_gather(picked, "section", axis=0, tiled=True)
    grad_all = (
        collected.reshape(sections, sections, capacity, features)
        .transpose(1, 0, 2, 3)
        .reshape(sections * slot_count, features)
    )
    returned = lax.dynamic_slice_in_dim(grad_all, section_id * slot_count, slot_count, 0)
    grad_own = returned.astype(jnp.float32)
    project_local = lax.dot_general(
        hidden, grad_all, (((0,), (0,)), ((), ())), preferred_element_type=jnp.float32
    )
    grad_hidden = lax.dot_general(
        grad_all, project_full, (((1,), (1,)), ((), ())), preferred_element_type=jnp.float32
    )
    grad_pre = (grad_hidden * derivative).astype(jnp.bfloat16)
    row_block = grad_pre
    grad_normed = lax.psum_scatter(
        lax.dot_general(
            row_block, expand_full, (((1,), (1,)), ((), ())), preferred_element_type=jnp.float32
        ).astype(jnp.bfloat16),
        "section",
        scatter_dimension=0,
        tiled=True,
    ).astype(jnp.float32)
    expand_local = lax.dot_general(
        gathered, grad_pre, (((0,), (0,)), ((), ())), preferred_element_type=jnp.float32
    )
    project_total, expand_total = (
        lax.psum(project_local.astype(jnp.bfloat16), "dp").astype(jnp.float32),
        lax.psum(expand_local.astype(jnp.bfloat16), "dp").astype(jnp.float32),
    )
    scaled_grad = grad_normed * gain
    centred = jnp.mean(scaled_grad * inputs, axis=-1, keepdims=True)
    grad_rows = (grad_own + inv_rms * scaled_grad - inputs * inv_rms**3 * centred).astype(
        jnp.bfloat16
    )
    return (
        embedded,
        grad_rows,
        expand_total.astype(jnp.bfloat16),
        project_total.astype(jnp.bfloat16),
    )


def solution(mesh):
    return jax.shard_map(
        shards,
        mesh=mesh,
        in_specs=(
            P(("dp", "section"), None),
            P(),
            P("dp", "section"),
            P("section", "dp"),
            P("dp", None),
            P(("dp", "section"), None),
            P(("dp", "section"), None),
            P(("dp", "section"), None),
        ),
        out_specs=(
            P(("dp", "section"), None),
            P(("dp", "section"), None),
            P(None, "section"),
            P("section", None),
        ),
        check_vma=False,
    )
```

profile of v0, /device:TPU:0, one launch (start us, length us, event | category | flops | bytes accessed | tf_op | source)
XLA Modules:
  0.0 686.7 jit_solution(13153148593107254716)
XLA Ops:
  7.2 0.0 copy-start
  7.2 0.0 all-gather.3.cloned.1.call-start
  7.2 0.7 all-gather.3.cloned.1.call-update
  7.9 0.0 all-gather.5.cloned.1.call-start
  8.0 0.7 all-gather.5.cloned.1.call-update
  8.7 0.0 all-reduce.9.cloned.1.call-start
  8.7 1.3 gather_fusion
  10.0 0.7 fusion.20
  10.7 0.0 copy-done
  10.7 0.6 gather_fusion.1
  11.3 0.1 broadcast_select_fusion
  11.4 6.4 all_gather.15
  17.8 0.1 copy.14
  17.9 0.1 reshape.120
  18.0 0.9 fusion.6
  18.9 0.8 fusion.8
  19.7 5.6 all_gather.12
  25.3 89.5 %all-gather.3.cloned.1.call-done = bf16[1600,2048]{1,0:T(8,128)(2,1)} async-done(((bf16[200,2048]{1,0:T(8,128)(2,1)}), bf16[1600,2048]{1,0:T(8,128)(2,1)}) %all-gather.3.cloned.1.call-update) | async-done | bytes 6553616 | tf_op jit(solution)/shard_map/all_gather | solution.py:28
  114.8 4.1 fusion.22
  118.9 4.7 convolution_convert_fusion
  123.6 93.5 %all-gather.5.cloned.1.call-done = bf16[2048,1600]{0,1:T(8,128)(2,1)} async-done(((bf16[2048,200]{0,1:T(8,128)(2,1)}), bf16[2048,1600]{0,1:T(8,128)(2,1)}) %all-gather.5.cloned.1.call-update) | async-done | bytes 6553616 | tf_op jit(solution)/shard_map/all_gather | solution.py:29
  217.1 0.0 copy-start.1
  217.1 5.7 convolution_convert_fusion.3
  222.8 0.0 copy-done.1
  222.8 1.3 fusion
  224.2 0.0 slice-done
  224.2 0.4 slice-done.1
  224.6 2.7 convolution_convert_fusion.2
  227.2 0.0 all-reduce.9.cloned.1.call-update
  227.2 0.0 all-reduce.7.cloned.1.call-start
  227.3 4.7 convolution_convert_fusion.1
  232.0 0.0 all-reduce.7.cloned.1.call-update
  232.0 0.6 copy-done.7
  232.6 0.6 dynamic-slice
  233.9 23.1 %all-reduce.9.cloned.1.call-done = (bf16[32,1600]{1,0:T(8,128)(2,1)}, bf16[32,1600]{1,0:T(8,128)(2,1)}) async-done(((bf16[32,1600]{1,0:T(8,128)(2,1)}, bf16[32,1600]{1,0:T(8,128)(2,1)}), (bf16[32,1600]{1,0:T(8,128)(2,1)}, bf16[32,1600]{1,0:T(8,128)(2,1)})) %all-reduce.9.cloned.1.call-update) | async-done | bytes 204816
  257.0 0.0 copy-done.3
  257.0 0.0 copy-done.6
  257.0 0.9 fusion.13
  257.9 1.5 fusion.12
  259.3 6.3 all_to_all.12
  265.6 0.0 copy-done.5
  265.6 0.8 scatter_custom_fusion
  266.5 0.0 copy-start.4
  266.5 403.8 %all-reduce.7.cloned.1.call-done = (bf16[1600,2048]{1,0:T(8,128)(2,1)}, bf16[2048,1600]{0,1:T(8,128)(2,1)}) async-done(((bf16[1600,2048]{1,0:T(8,128)(2,1)}, bf16[2048,1600]{0,1:T(8,128)(2,1)}), (bf16[1600,2048]{1,0:T(8,128)(2,1)}, bf16[2048,1600]{0,1:T(8,128)(2,1)})) %all-reduce.7.cloned.1.call-update) | async-done | bytes 13107216 | tf_op jit(solution)/shard_map/psum | solution.py:81
  670.3 7.0 %copy.22 = bf16[1600,2048]{1,0:T(8,128)(2,1)} copy(bf16[1600,2048]{1,0:T(8,128)(2,1)} %get-tuple-element.14) | data formatting | bytes 13107200
  677.3 0.0 copy-done.4
  677.3 0.0 copy-done.2
  677.3 2.8 copy.23
  (17 shorter events, 0.2 us)
Async XLA Ops:
  7.2 3.6 copy-start
  7.2 107.6 %all-gather.3.cloned.1.call-start = ((), (), s32[]{:S(2)}) async-start(), calls=%async_computation.1 | async-start | bytes 7372800 | tf_op jit(solution)/shard_map/all_gather | solution.py:28
  7.9 209.2 %all-gather.5.cloned.1.call-start = ((), (), s32[]{:S(2)}) async-start(), calls=%async_computation.2 | async-start | bytes 7372800 | tf_op jit(solution)/shard_map/all_gather | solution.py:29
  8.7 248.3 %all-reduce.9.cloned.1.call-start = ((), (), s32[]{:S(2)}) async-start(), calls=%async_computation.4 | async-start | bytes 425984
  217.1 5.7 copy-start.1
  217.1 7.0 %slice-start = ((s8[6553600]{0:T(1024)(128)(4,1)}), s8[4194304]{0:T(1024)(128)(4,1)S(1)}, s32[]{:S(2)}) async-start(s8[6553600]{0:T(1024)(128)(4,1)} %bitcast.21), calls=%async_computation.5 | async-start | bytes 8388608
  222.8 1.7 slice-start.1
  227.2 443.1 %all-reduce.7.cloned.1.call-start = ((), (), s32[]{:S(2)}) async-start(), calls=%async_computation.3 | async-start | bytes 26214400 | tf_op jit(solution)/shard_map/psum | solution.py:81
  232.0 0.7 copy-start.7
  232.0 25.0 %copy-start.3 = (bf16[8,1600]{1,0:T(8,128)(2,1)S(1)}, bf16[8,1600]{1,0:T(8,128)(2,1)}, u32[]{:S(2)}) copy-start(bf16[8,1600]{1,0:T(8,128)(2,1)} %param.8) | copy-start | bytes 76804
  232.0 25.0 %copy-start.6 = (f32[1600]{0:T(1024)S(1)}, f32[1600]{0:T(1024)}, u32[]{:S(2)}) copy-start(f32[1600]{0:T(1024)} %param.9) | copy-start | bytes 19204
  232.0 33.7 %copy-start.5 = (bf16[16,1600]{1,0:T(8,128)(2,1)S(1)}, bf16[16,1600]{1,0:T(8,128)(2,1)}, u32[]{:S(2)}) copy-start(bf16[16,1600]{1,0:T(8,128)(2,1)} %param.14) | copy-start | bytes 153604
  266.5 410.8 %copy-start.4 = (bf16[16,1600]{1,0:T(8,128)(2,1)}, bf16[16,1600]{1,0:T(8,128)(2,1)S(1)}, u32[]{:S(2)}) copy-start(bf16[16,1600]{1,0:T(8,128)(2,1)S(1)} %scatter_custom_fusion) | copy-start | bytes 153604
  670.3 7.0 %copy-start.2 = (bf16[2048,1600]{0,1:T(8,128)(2,1)S(1)}, bf16[2048,1600]{0,1:T(8,128)(2,1)}, u32[]{:S(2)}) copy-start(bf16[2048,1600]{0,1:T(8,128)(2,1)} %get-tuple-element.15) | copy-start | bytes 19660804
Sparse Core Ops, SparseCore 0:
  10.2 104.6 all-gather.2
  117.0 100.0 all-gather.4
  227.4 29.5 all-reduce.8
  261.7 408.5 all-reduce.6
where the time goes:
time: 687 us
  waiting for transfers between devices  611 us (89%)
  matrix products  23.2 us (3%)
  blocking collectives  18.2 us (3%)
  between operations  14.5 us (2%)
  local copies, waits for them, and re-layouts  13.6 us (2%)
    psum x1, waiting for transfers between devices, shards(): lax.psum(expand_local.astype(jnp.bfloat16), 'dp').astype(jnp.float32)  404 us
    all_gather x1, waiting for transfers between devices, shards(): lax.all_gather(project_weight, 'dp', axis=1, tiled=True)  93.5 us
    all_gather x1, waiting for transfers between devices, shards(): lax.all_gather(expand_weight, 'dp', axis=0, tiled=True)  89.5 us
    unnamed x5, waiting for transfers between devices  24.5 us
  transfers between devices with their start and end apart: 4, of which 4 were waited for; matrix products, arithmetic and copies ran while one was open for 3% of the time, Pallas kernels for 0%

commit v1 on v0

--- a/solution.py
+++ b/solution.py
@@ -15,7 +15,9 @@
     return (activated, derivative)
 
 
-def shards(patches, gain, expand_weight, project_weight, counts, positions, text, cotangent):
+def gather_weights_plan(
+    patches, gain, expand_weight, project_weight, counts, positions, text, cotangent
+):
     sections = lax.axis_size("section")
     slot_count = patches.shape[0]
     features = patches.shape[1]
@@ -93,6 +95,152 @@
     )
 
 
+def exchange_bits(size):
+    bits = []
+    step = 1
+    while step < size:
+        bits.append(step)
+        step *= 2
+    return bits
+
+
+def swap(array, axis, step):
+    size = lax.axis_size(axis)
+    return lax.ppermute(array, axis, [(i, i ^ step) for i in range(size)])
+
+
+def doubling_gather(array, axis, steps):
+    me = lax.axis_index(axis)
+    held = array.reshape((1,) * len(steps) + array.shape)
+    for step in steps:
+        level = len(steps) - 1 - (step.bit_length() - 1)
+        got = swap(held, axis, step)
+        high = (me // step) % 2 == 1
+        held = jnp.where(
+            high,
+            jnp.concatenate([got, held], axis=level),
+            jnp.concatenate([held, got], axis=level),
+        )
+    return held.reshape((lax.axis_size(axis),) + array.shape)
+
+
+def move_rows_plan(
+    patches, gain, expand_weight, project_weight, counts, positions, text, cotangent
+):
+    sections = lax.axis_size("section")
+    replicas = lax.axis_size("dp")
+    devices = sections * replicas
+    slot_count, features = patches.shape
+    part = expand_weight.shape[0]
+    capacity = slot_count // sections
+    rows = devices * slot_count
+    section_id = lax.axis_index("section")
+    replica_id = lax.axis_index("dp")
+
+    expand_slice = lax.all_to_all(expand_weight, "dp", split_axis=1, concat_axis=0, tiled=True)
+    project_slice = lax.all_to_all(project_weight, "dp", split_axis=0, concat_axis=1, tiled=True)
+
+    arrival = jnp.arange(slot_count, dtype=jnp.int32)
+    slot_index = section_id * capacity + arrival % capacity
+    is_live = slot_index < jnp.repeat(counts[0], capacity)
+    spots = jnp.arange(text.shape[0], dtype=jnp.int32)
+    lands = (positions[0][:, None] == spots[None, :]) & is_live[:, None]
+    chooser = lands.astype(jnp.bfloat16)
+    picked = jnp.dot(chooser, cotangent, preferred_element_type=jnp.float32).astype(jnp.bfloat16)
+
+    pair = jnp.concatenate([patches, picked], axis=0)
+    over_dp = doubling_gather(pair, "dp", exchange_bits(replicas)[::-1])
+    over_all = doubling_gather(over_dp, "section", exchange_bits(sections)[::-1])
+    over_all = over_all.reshape(sections, replicas, 2, slot_count, features)
+    inputs_all = over_all[:, :, 0].transpose(1, 0, 2, 3).reshape(rows, features)
+    grad_all = (
+        over_all[:, :, 1]
+        .reshape(sections, replicas, sections, capacity, features)
+        .transpose(1, 2, 0, 3, 4)
+        .reshape(rows, features)
+    )
+
+    wide = inputs_all.astype(jnp.float32)
+    inv_rms_all = lax.rsqrt(jnp.mean(wide * wide, axis=-1, keepdims=True) + 1e-06)
+    normed = (wide * inv_rms_all * gain).astype(jnp.bfloat16)
+
+    preact = jnp.dot(normed, expand_slice, preferred_element_type=jnp.float32)
+    activated, derivative = gelu_pair(preact)
+    hidden_part = activated.astype(jnp.bfloat16)
+    grad_hidden = lax.dot_general(
+        grad_all, project_slice, (((1,), (1,)), ((), ())), preferred_element_type=jnp.float32
+    )
+    grad_pre_part = (grad_hidden * derivative).astype(jnp.bfloat16)
+
+    both = jnp.stack([hidden_part, grad_pre_part])
+    spread = doubling_gather(both, "dp", exchange_bits(replicas)[::-1])
+    spread = spread.transpose(1, 2, 0, 3).reshape(2, rows, -1)
+    hidden, grad_pre = spread[0], spread[1]
+
+    mixed_part = jnp.dot(hidden, project_weight, preferred_element_type=jnp.float32)
+    grad_normed_part = lax.dot_general(
+        grad_pre, expand_weight, (((1,), (1,)), ((), ())), preferred_element_type=jnp.float32
+    )
+    mixed_part = (
+        mixed_part.astype(jnp.bfloat16)
+        .reshape(replicas, sections, sections, capacity, part)
+        .transpose(0, 2, 1, 3, 4)
+        .reshape(devices, slot_count, part)
+    )
+    grad_normed_part = grad_normed_part.astype(jnp.bfloat16).reshape(devices, slot_count, part)
+    tail = jnp.concatenate([mixed_part, grad_normed_part], axis=1)
+    tail = lax.all_to_all(tail, ("dp", "section"), split_axis=0, concat_axis=0, tiled=True)
+    tail = tail.reshape(replicas, sections, 2 * slot_count, part).astype(jnp.float32)
+    tail = jnp.sum(tail, axis=1).transpose(1, 0, 2).reshape(2 * slot_count, features)
+    mixed, grad_normed = tail[:slot_count], tail[slot_count:]
+
+    expand_grad = lax.dot_general(
+        normed, grad_pre, (((0,), (0,)), ((), ())), preferred_element_type=jnp.float32
+    ).astype(jnp.bfloat16)
+    project_grad = lax.dot_general(
+        hidden, grad_all, (((0,), (0,)), ((), ())), preferred_element_type=jnp.float32
+    ).astype(jnp.bfloat16)
+
+    group = sections * slot_count
+    mine = lax.dynamic_slice_in_dim(inputs_all, replica_id * group, group, 0)
+    mine = mine.reshape(sections, sections, capacity, features)
+    coming = lax.dynamic_index_in_dim(mine, section_id, 1, keepdims=False)
+    coming = coming.reshape(slot_count, features)
+    out_rows = (coming.astype(jnp.float32) + mixed).astype(jnp.bfloat16)
+    placed = lax.dot_general(
+        chooser, out_rows, (((0,), (0,)), ((), ())), preferred_element_type=jnp.float32
+    ).astype(jnp.bfloat16)
+    taken = jnp.any(lands, axis=0)[:, None]
+    embedded = jnp.where(taken, placed, text)
+
+    inputs = patches.astype(jnp.float32)
+    inv_rms = lax.rsqrt(jnp.mean(inputs * inputs, axis=-1, keepdims=True) + 1e-06)
+    grad_own = lax.dynamic_slice_in_dim(
+        grad_all, (replica_id * sections + section_id) * slot_count, slot_count, 0
+    ).astype(jnp.float32)
+    scaled_grad = grad_normed * gain
+    centred = jnp.mean(scaled_grad * inputs, axis=-1, keepdims=True)
+    grad_rows = (grad_own + inv_rms * scaled_grad - inputs * inv_rms**3 * centred).astype(
+        jnp.bfloat16
+    )
+    return (embedded, grad_rows, expand_grad, project_grad)
+
+
+def shards(patches, gain, expand_weight, project_weight, counts, positions, text, cotangent):
+    replicas, sections = lax.axis_size("dp"), lax.axis_size("section")
+    slot_count, features = patches.shape
+    units = expand_weight.shape[1]
+    rows = replicas * sections * slot_count
+    powers = replicas & (replicas - 1) == 0 and sections & (sections - 1) == 0
+    if powers and units % replicas == 0 and rows * (features + units) <= features * units:
+        plan = move_rows_plan
+    else:
+        plan = gather_weights_plan
+    return plan(
+        patches, gain, expand_weight, project_weight, counts, positions, text, cotangent
+    )
+
+
 def solution(mesh):
     return jax.shard_map(
         shards,

time: 687 us -> 158 us (0.23)
  waiting for transfers between devices: 611 us -> 91.9 us
  starting transfers between devices: 0.16 us -> 25.1 us
  blocking collectives: 18.2 us -> 0 us
  between operations: 14.5 us -> 1.05 us
    psum x1 -> x0, waiting for transfers between devices: 404 us -> none  [shards(): lax.psum(expand_local.astype(jnp.bfloat16), 'dp').astype(jnp.float32)]
    all_gather x2 -> x0, waiting for transfers between devices: 183 us -> none  [the longest x1 93.5 us: shards(): lax.all_gather(project_weight, 'dp', axis=1, tiled=True)]
    ppermute x0 -> x8, waiting for transfers between devices: none -> 58.4 us  [swap(): return lax.ppermute(array, axis, [(i, i ^ step) for i in range(size)])]
    all_to_all x0 -> x3, waiting for transfers between devices: none -> 33.5 us  [the longest x1 15 us: move_rows_plan(): lax.all_to_all(project_weight, 'dp', split_axis=0, concat_axis=1, tiled=T...]
    unnamed x5 -> x0, waiting for transfers between devices: 24.5 us -> none
    all_to_all x0 -> x3, starting transfers between devices: none -> 12.8 us  [the longest x1 5.94 us: move_rows_plan(): lax.all_to_all(expand_weight, 'dp', split_axis=1, concat_axis=0, tiled=True)]
    ppermute x0 -> x8, starting transfers between devices: none -> 12.3 us  [swap(): return lax.ppermute(array, axis, [(i, i ^ step) for i in range(size)])]
    all_gather x2 -> x0, blocking collectives: 12 us -> none  [the longest x1 6.39 us: shards(): collected = lax.all_gather(picked, 'section', axis=0, tiled=True)]
  transfers between devices with their start and end apart: 4 -> 11, of which waited for: 4 -> 10; matrix products, arithmetic and copies ran while one was open for 3% -> 8% of each run, Pallas kernels for 0% -> 0%
where the time goes in v1:
time: 158 us; the launch traced here: 157 us
  waiting for transfers between devices  91.9 us (58%)
  starting transfers between devices  25.1 us (16%)
  matrix products  17.7 us (11%)
  local copies, waits for them, and re-layouts  12.3 us (8%)
  other arithmetic  9.01 us (6%)
    ppermute x8, waiting for transfers between devices, swap(): return lax.ppermute(array, axis, [(i, i ^ step) for i in range(size)])  58.4 us
    all_to_all x1, waiting for transfers between devices, move_rows_plan(): lax.all_to_all(project_weight, 'dp', split_axis=0, concat_axis=1, tiled=T...  15 us
    all_to_all x1, waiting for transfers between devices, move_rows_plan(): lax.all_to_all(expand_weight, 'dp', split_axis=1, concat_axis=0, tiled=True)  12.8 us
    ppermute x8, starting transfers between devices, swap(): return lax.ppermute(array, axis, [(i, i ^ step) for i in range(size)])  12.3 us
    all_to_all x1, starting transfers between devices, move_rows_plan(): lax.all_to_all(expand_weight, 'dp', split_axis=1, concat_axis=0, tiled=True)  5.94 us
    all_to_all x1, waiting for transfers between devices, move_rows_plan(): lax.all_to_all(tail, ('dp', 'section'), split_axis=0, concat_axis=0, tile...  5.71 us
    select_n x8, other arithmetic, doubling_gather(): jnp.where(high, jnp.concatenate([got, held], axis=level), jnp.concatenate...  4.98 us
    dot_general x1, matrix products, move_rows_plan(): lax.dot_general(normed, grad_pre, (((0,), (0,)), ((), ())), preferred_ele...  4.84 us
  transfers between devices with their start and end apart: 11, of which 10 were waited for; matrix products, arithmetic and copies ran while one was open for 8% of the time, Pallas kernels for 0%

profile of v1, /device:TPU:0, one launch (start us, length us, event | category | flops | bytes accessed | tf_op | source)
XLA Modules:
  0.0 157.1 jit_solution(18436717894969461480)
XLA Ops:
  0.7 0.8 broadcast_in_dim.7
  1.6 0.8 convolution_convert_fusion.3
  2.4 0.8 fusion.22
  3.2 4.1 %collective-permute-start = (bf16[1,1,1,16,1600]{4,3,0,2,1:T(8,128)(2,1)S(1)}, bf16[1,1,1,16,1600]{4,3,0,2,1:T(8,128)(2,1)S(1)}, u32[]{:S(2)}, u32[]{:S(2)}) collective-permute-start(bf16[1,1,1,16,1600]{4,3,0,2,1:T(8,128)(2,1)S(1)} %get-tuple-element.14), channel_id=1, source_target_pairs={{0,16},{4,20},{8,24},{12,28},{16,0},{20,4},{24,8},{28,12},{1,17},{... | collective-permute-start | bytes 153608 | tf_op jit(solution)/shard_map/ppermute | solution.py:109
  7.2 2.7 %collective-permute-done = bf16[1,1,1,16,1600]{4,3,0,2,1:T(8,128)(2,1)S(1)} collective-permute-done((bf16[1,1,1,16,1600]{4,3,0,2,1:T(8,128)(2,1)S(1)}, bf16[1,1,1,16,1600]{4,3,0,2,1:T(8,128)(2,1)S(1)}, u32[]{:S(2)}, u32[]{:S(2)}) %collective-permute-start) | collective-permute-done | bytes 51232 | tf_op jit(solution)/shard_map/ppermute | solution.py:109
  9.9 1.4 collective-permute-start.1
  11.4 3.3 %collective-permute-done.1 = bf16[2,1,1,16,1600]{4,3,0,2,1:T(8,128)(2,1)S(1)} collective-permute-done((bf16[2,1,1,16,1600]{4,3,0,2,1:T(8,128)(2,1)S(1)}, bf16[2,1,1,16,1600]{4,3,0,2,1:T(8,128)(2,1)S(1)}, u32[]{:S(2)}, u32[]{:S(2)}) %collective-permute-start.1) | collective-permute-done | bytes 102432 | tf_op jit(solution)/shard_map/ppermute | solution.py:109
  14.8 1.8 %collective-permute-start.2 = (bf16[2,2,1,16,1600]{4,3,0,2,1:T(8,128)(2,1)S(1)}, bf16[2,2,1,16,1600]{4,3,0,2,1:T(8,128)(2,1)S(1)}, u32[]{:S(2)}, u32[]{:S(2)}) collective-permute-start(bf16[2,2,1,16,1600]{4,3,0,2,1:T(8,128)(2,1)S(1)} %maximum_select_fusion.7), channel_id=1, source_target_pairs={{0,4},{4,0},{8,12},{12,8},{16,20},{20,16},{24,28},{28,24},{1,5},{5... | collective-permute-start | bytes 614408 | tf_op jit(solution)/shard_map/ppermute | solution.py:109
  16.5 4.1 %collective-permute-done.2 = bf16[2,2,1,16,1600]{4,3,0,2,1:T(8,128)(2,1)S(1)} collective-permute-done((bf16[2,2,1,16,1600]{4,3,0,2,1:T(8,128)(2,1)S(1)}, bf16[2,2,1,16,1600]{4,3,0,2,1:T(8,128)(2,1)S(1)}, u32[]{:S(2)}, u32[]{:S(2)}) %collective-permute-start.2) | collective-permute-done | bytes 204832 | tf_op jit(solution)/shard_map/ppermute | solution.py:109
  20.8 1.8 %collective-permute-start.3 = (bf16[1,1,8,16,1600]{4,3,2,1,0:T(8,128)(2,1)S(1)}, bf16[1,1,8,16,1600]{4,3,2,1,0:T(8,128)(2,1)S(1)}, u32[]{:S(2)}, u32[]{:S(2)}) collective-permute-start(bf16[1,1,8,16,1600]{4,3,2,1,0:T(8,128)(2,1)S(1)} %bitcast.82), channel_id=1, source_target_pairs={{0,2},{1,3},{2,0},{3,1},{4,6},{5,7},{6,4},{7,5},{8,10},{9,11},{10,... | collective-permute-start | bytes 1228808 | tf_op jit(solution)/shard_map/ppermute | solution.py:109
  22.6 0.9 copy.83
  23.5 5.9 %all-to-all-start = ((bf16[200,8,256]{2,0,1:T(8,128)(2,1)}), bf16[200,8,256]{2,0,1:T(8,128)(2,1)}, u32[]{:S(2)}, u32[]{:S(2)}) async-start(bf16[200,8,256]{2,0,1:T(8,128)(2,1)} %bitcast.70), calls=%async_computation | async-start | bytes 1638400 | tf_op jit(solution)/shard_map/all_to_all | solution.py:140
  29.5 0.2 maximum_select_fusion.3
  29.8 0.9 copy.82
  30.7 1.5 collective-permute-done.4
  32.2 1.8 %maximum_select_fusion.1 = bf16[2,2,8,16,1600]{4,3,2,1,0:T(8,128)(2,1)S(1)} fusion(bf16[2,1,8,16,1600]{4,3,2,1,0:T(8,128)(2,1)S(1)} %maximum_select_fusion.3, bf16[2,1,8,16,1600]{4,3,2,1,0:T(8,128)(2,1)} %collective-permute-done.4, pred[]{:T(512)S(6)} %eq.48), kind=kLoop, calls=%fused_computation.11 | loop fusion | flops 2457600 | bytes 3276801 | tf_op jit(solution)/shard_map/jit(_where)/select_n | solution.py:119
  34.0 12.8 %all-to-all-done = bf16[200,8,256]{2,0,1:T(8,128)(2,1)} async-done(((bf16[200,8,256]{2,0,1:T(8,128)(2,1)}), bf16[200,8,256]{2,0,1:T(8,128)(2,1)}, u32[]{:S(2)}, u32[]{:S(2)}) %all-to-all-start) | async-done | bytes 819232 | tf_op jit(solution)/shard_map/all_to_all | solution.py:140
  46.8 4.2 %all-to-all-start.1 = ((bf16[8,256,200]{1,2,0:T(8,128)(2,1)}), bf16[8,256,200]{1,2,0:T(8,128)(2,1)}, u32[]{:S(2)}, u32[]{:S(2)}) async-start(bf16[8,256,200]{1,2,0:T(8,128)(2,1)} %bitcast.69), calls=%async_computation.1 | async-start | bytes 1638400 | tf_op jit(solution)/shard_map/all_to_all | solution.py:141
  51.1 0.1 fusion.34
  51.3 0.7 copy.64
  52.0 0.7 reshape.706
  52.7 0.3 fusion.1
  52.9 0.3 fusion.3
  53.2 1.6 %fusion.36 = f32[256,256]{0,1:T(8,128)S(1)} fusion(bf16[256,1600]{1,0:T(8,128)(2,1)S(1)} %bitcast.73, bf16[1600,256]{1,0:T(8,128)(2,1)} %bitcast.14), kind=kOutput, calls=%fused_computation.74 | convolution fusion | flops 209715200 | bytes 1900544 | tf_op jit(solution)/shard_map/dot_general | solution.py:167
  54.9 15.0 %all-to-all-done.1 = bf16[8,256,200]{1,2,0:T(8,128)(2,1)} async-done(((bf16[8,256,200]{1,2,0:T(8,128)(2,1)}), bf16[8,256,200]{1,2,0:T(8,128)(2,1)}, u32[]{:S(2)}, u32[]{:S(2)}) %all-to-all-start.1) | async-done | bytes 819232 | tf_op jit(solution)/shard_map/all_to_all | solution.py:141
  69.9 1.7 %fusion.5 = bf16[1,256,256]{1,2,0:T(8,128)(2,1)S(1)} fusion(bf16[256,1600]{1,0:T(8,128)(2,1)S(1)} %reshape.706, bf16[256,1600]{0,1:T(8,128)(2,1)} %bitcast.19, f32[256,256]{0,1:T(8,128)S(1)} %fusion.36), kind=kOutput, calls=%fused_computation.16 | convolution fusion | flops 210960384 | bytes 2031616 | tf_op jit(solution)/shard_map/dot_general | solution.py:170
  71.6 0.3 collective-permute-start.5
  71.9 11.5 %collective-permute-done.5 = bf16[1,1,1,2,256,256]{4,5,3,0,2,1:T(8,128)(2,1)S(1)} collective-permute-done((bf16[1,1,1,2,256,256]{4,5,3,0,2,1:T(8,128)(2,1)S(1)}, bf16[1,1,1,2,256,256]{4,5,3,0,2,1:T(8,128)(2,1)S(1)}, u32[]{:S(2)}, u32[]{:S(2)}) %collective-permute-start.5) | collective-permute-done | bytes 262176 | tf_op jit(solution)/shard_map/ppermute | solution.py:109
  83.7 12.9 %collective-permute-done.6 = bf16[2,1,1,2,256,256]{4,5,3,0,2,1:T(8,128)(2,1)S(1)} collective-permute-done((bf16[2,1,1,2,256,256]{4,5,3,0,2,1:T(8,128)(2,1)S(1)}, bf16[2,1,1,2,256,256]{4,5,3,0,2,1:T(8,128)(2,1)S(1)}, u32[]{:S(2)}, u32[]{:S(2)}) %collective-permute-start.6) | collective-permute-done | bytes 524320 | tf_op jit(solution)/shard_map/ppermute | solution.py:109
  96.6 0.2 maximum_select_fusion.2
  96.8 2.8 %collective-permute-start.7 = (bf16[2,2,1,2,256,256]{4,5,3,0,2,1:T(8,128)(2,1)S(1)}, bf16[2,2,1,2,256,256]{4,5,3,0,2,1:T(8,128)(2,1)}, u32[]{:S(2)}, u32[]{:S(2)}) collective-permute-start(bf16[2,2,1,2,256,256]{4,5,3,0,2,1:T(8,128)(2,1)S(1)} %maximum_select_fusion.2), channel_id=1, source_target_pairs={{0,4},{4,0},{8,12},{12,8},{16,20},{20,16},{24,28},{28,24},{1,5},{5... | collective-permute-start | bytes 3145736 | tf_op jit(solution)/shard_map/ppermute | solution.py:109
  99.9 22.3 %collective-permute-done.7 = bf16[2,2,1,2,256,256]{4,5,3,0,2,1:T(8,128)(2,1)} collective-permute-done((bf16[2,2,1,2,256,256]{4,5,3,0,2,1:T(8,128)(2,1)S(1)}, bf16[2,2,1,2,256,256]{4,5,3,0,2,1:T(8,128)(2,1)}, u32[]{:S(2)}, u32[]{:S(2)}) %collective-permute-start.7) | collective-permute-done | bytes 1048608 | tf_op jit(solution)/shard_map/ppermute | solution.py:109
  122.2 2.7 %maximum_select_fusion = bf16[2,2,2,2,256,256]{4,5,3,0,2,1:T(8,128)(2,1)S(1)} fusion(bf16[2,2,1,2,256,256]{4,5,3,0,2,1:T(8,128)(2,1)} %copy-done.1, bf16[2,2,1,2,256,256]{4,5,3,0,2,1:T(8,128)(2,1)} %collective-permute-done.7, pred[]{:T(512)S(6)} %eq.50), kind=kLoop, calls=%fused_computation.7 | loop fusion | flops 3145728 | bytes 4194305 | tf_op jit(solution)/shard_map/jit(_where)/select_n | solution.py:119
  124.9 2.3 %copy.66 = bf16[2,2,2,2,256,256]{5,4,3,2,1,0:T(8,128)(2,1)} copy(bf16[2,2,2,2,256,256]{4,5,3,0,2,1:T(8,128)(2,1)S(1)} %maximum_select_fusion) | data formatting | bytes 4194304 | tf_op jit(solution)/shard_map/jit(_where)/select_n | solution.py:119
  127.2 2.7 %fusion.33 = (bf16[1,256,8,256]{3,1,0,2:T(8,128)(2,1)}, bf16[1,256,8,256]{3,1,0,2:T(8,128)(2,1)S(1)}) fusion(bf16[2,256,8,256]{3,1,0,2:T(8,128)(2,1)} %bitcast.77), kind=kLoop, calls=%fused_computation.71 | loop fusion | bytes 4194304 | tf_op jit(solution)/shard_map/slice | solution.py:178
  129.9 1.5 copy.67
  131.4 1.6 %convolution_convert_fusion.5 = bf16[256,200]{0,1:T(8,128)(2,1)S(1)} fusion(bf16[256,2048]{0,1:T(8,128)(2,1)S(1)} %bitcast.71, bf16[2048,200]{0,1:T(8,128)(2,1)} %param.11), kind=kOutput, calls=%fused_computation.15 | convolution fusion | flops 209766400 | bytes 1970176 | tf_op jit(solution)/shard_map/dot_general | solution.py:180
  133.0 4.7 %convolution_convert_fusion = bf16[2048,1600]{0,1:T(8,128)(2,1)} fusion(bf16[256,2048]{0,1:T(8,128)(2,1)S(1)} %bitcast.72, bf16[256,1600]{1,0:T(8,128)(2,1)S(1)} %copy-done.3), kind=kOutput, calls=%fused_computation | convolution fusion | flops 1680998400 | bytes 8421376 | tf_op jit(solution)/shard_map/dot_general | solution.py:200
  138.0 0.1 reshape.709
  138.1 0.5 copy.70
  138.7 1.5 convolution_convert_fusion.4
  140.3 0.7 pad_maximum_fusion.1
  141.1 2.6 %all-to-all-start.2 = ((bf16[32,16,200]{2,1,0:T(8,128)(2,1)}), bf16[32,16,200]{2,1,0:T(8,128)(2,1)S(1)}, u32[]{:S(2)}, u32[]{:S(2)}) async-start(bf16[32,16,200]{2,1,0:T(8,128)(2,1)} %pad_maximum_fusion.1), calls=%async_computation.2 | async-start | bytes 524288 | tf_op jit(solution)/shard_map/all_to_all | solution.py:192
  143.7 4.8 %convolution_convert_fusion.1 = bf16[1600,2048]{1,0:T(8,128)(2,1)} fusion(bf16[256,1600]{1,0:T(8,128)(2,1)S(1)} %bitcast.74, bf16[256,2048]{0,1:T(8,128)(2,1)S(1)} %bitcast.76), kind=kOutput, calls=%fused_computation.1 | convolution fusion | flops 1680998400 | bytes 8421376 | tf_op jit(solution)/shard_map/dot_general | solution.py:197
  148.5 5.7 %all-to-all-done.2 = bf16[32,16,200]{2,1,0:T(8,128)(2,1)S(1)} async-done(((bf16[32,16,200]{2,1,0:T(8,128)(2,1)}), bf16[32,16,200]{2,1,0:T(8,128)(2,1)S(1)}, u32[]{:S(2)}, u32[]{:S(2)}) %all-to-all-start.2) | async-done | bytes 204832 | tf_op jit(solution)/shard_map/all_to_all | solution.py:192
  154.4 0.2 fusion.16
  154.7 1.4 fusion.19
  156.2 0.9 fusion
  (53 shorter events, 1.8 us)
Async XLA Ops:
  0.6 0.9 copy-start
  0.6 21.9 %copy-start.5 = (bf16[200,2048]{1,0:T(8,128)(2,1)S(1)}, bf16[200,2048]{1,0:T(8,128)(2,1)}, u32[]{:S(2)}) copy-start(bf16[200,2048]{1,0:T(8,128)(2,1)} %param.10) | copy-start | bytes 2457604
  3.2 6.7 %collective-permute-start = (bf16[1,1,1,16,1600]{4,3,0,2,1:T(8,128)(2,1)S(1)}, bf16[1,1,1,16,1600]{4,3,0,2,1:T(8,128)(2,1)S(1)}, u32[]{:S(2)}, u32[]{:S(2)}) collective-permute-start(bf16[1,1,1,16,1600]{4,3,0,2,1:T(8,128)(2,1)S(1)} %get-tuple-element.14), channel_id=1, source_target_pairs={{0,16},{4,20},{8,24},{12,28},{16,0},{20,4},{24,8},{28,12},{1,17},{... | collective-permute-start | bytes 153608 | tf_op jit(solution)/shard_map/ppermute | solution.py:109
  9.9 4.8 %collective-permute-start.1 = (bf16[2,1,1,16,1600]{4,3,0,2,1:T(8,128)(2,1)S(1)}, bf16[2,1,1,16,1600]{4,3,0,2,1:T(8,128)(2,1)S(1)}, u32[]{:S(2)}, u32[]{:S(2)}) collective-permute-start(bf16[2,1,1,16,1600]{4,3,0,2,1:T(8,128)(2,1)S(1)} %maximum_select_fusion.8), channel_id=1, source_target_pairs={{0,8},{4,12},{8,0},{12,4},{16,24},{20,28},{24,16},{28,20},{1,9},{5... | collective-permute-start | bytes 307208 | tf_op jit(solution)/shard_map/ppermute | solution.py:109
  14.8 5.9 %collective-permute-start.2 = (bf16[2,2,1,16,1600]{4,3,0,2,1:T(8,128)(2,1)S(1)}, bf16[2,2,1,16,1600]{4,3,0,2,1:T(8,128)(2,1)S(1)}, u32[]{:S(2)}, u32[]{:S(2)}) collective-permute-start(bf16[2,2,1,16,1600]{4,3,0,2,1:T(8,128)(2,1)S(1)} %maximum_select_fusion.7), channel_id=1, source_target_pairs={{0,4},{4,0},{8,12},{12,8},{16,20},{20,16},{24,28},{28,24},{1,5},{5... | collective-permute-start | bytes 614408 | tf_op jit(solution)/shard_map/ppermute | solution.py:109
  20.8 8.7 %collective-permute-start.3 = (bf16[1,1,8,16,1600]{4,3,2,1,0:T(8,128)(2,1)S(1)}, bf16[1,1,8,16,1600]{4,3,2,1,0:T(8,128)(2,1)S(1)}, u32[]{:S(2)}, u32[]{:S(2)}) collective-permute-start(bf16[1,1,8,16,1600]{4,3,2,1,0:T(8,128)(2,1)S(1)} %bitcast.82), channel_id=1, source_target_pairs={{0,2},{1,3},{2,0},{3,1},{4,6},{5,7},{6,4},{7,5},{8,10},{9,11},{10,... | collective-permute-start | bytes 1228808 | tf_op jit(solution)/shard_map/ppermute | solution.py:109
  23.5 6.2 %copy-start.4 = (bf16[2048,200]{0,1:T(8,128)(2,1)S(1)}, bf16[2048,200]{0,1:T(8,128)(2,1)}, u32[]{:S(2)}) copy-start(bf16[2048,200]{0,1:T(8,128)(2,1)} %param.11) | copy-start | bytes 2457604
  23.5 23.3 %all-to-all-start = ((bf16[200,8,256]{2,0,1:T(8,128)(2,1)}), bf16[200,8,256]{2,0,1:T(8,128)(2,1)}, u32[]{:S(2)}, u32[]{:S(2)}) async-start(bf16[200,8,256]{2,0,1:T(8,128)(2,1)} %bitcast.70), calls=%async_computation | async-start | bytes 1638400 | tf_op jit(solution)/shard_map/all_to_all | solution.py:140
  29.6 2.6 %collective-permute-start.4 = (bf16[2,1,8,16,1600]{4,3,2,1,0:T(8,128)(2,1)S(1)}, bf16[2,1,8,16,1600]{4,3,2,1,0:T(8,128)(2,1)}, u32[]{:S(2)}, u32[]{:S(2)}) collective-permute-start(bf16[2,1,8,16,1600]{4,3,2,1,0:T(8,128)(2,1)S(1)} %maximum_select_fusion.3), channel_id=1, source_target_pairs={{0,1},{1,0},{2,3},{3,2},{4,5},{5,4},{6,7},{7,6},{8,9},{9,8},{10,11... | collective-permute-start | bytes 2457608 | tf_op jit(solution)/shard_map/ppermute | solution.py:109
  46.8 23.1 %all-to-all-start.1 = ((bf16[8,256,200]{1,2,0:T(8,128)(2,1)}), bf16[8,256,200]{1,2,0:T(8,128)(2,1)}, u32[]{:S(2)}, u32[]{:S(2)}) async-start(bf16[8,256,200]{1,2,0:T(8,128)(2,1)} %bitcast.69), calls=%async_computation.1 | async-start | bytes 1638400 | tf_op jit(solution)/shard_map/all_to_all | solution.py:141
  51.3 1.6 %copy-start.7 = (f32[1600]{0:T(1024)S(1)}, f32[1600]{0:T(1024)}, u32[]{:S(2)}) copy-start(f32[1600]{0:T(1024)} %param.9) | copy-start | bytes 19204
  52.6 17.3 %copy-start.2 = (bf16[256,1600]{1,0:T(8,128)(2,1)}, bf16[256,1600]{1,0:T(8,128)(2,1)S(1)}, u32[]{:S(2)}) copy-start(bf16[256,1600]{1,0:T(8,128)(2,1)S(1)} %reshape.706) | copy-start | bytes 2457604
  71.6 28.0 %copy-start.9 = (s32[1,8]{1,0:T(1,128)S(1)}, s32[1,8]{1,0:T(1,128)}, u32[]{:S(2)}) copy-start(s32[1,8]{1,0:T(1,128)} %param.13) | copy-start | bytes 100
  71.6 11.8 %collective-permute-start.5 = (bf16[1,1,1,2,256,256]{4,5,3,0,2,1:T(8,128)(2,1)S(1)}, bf16[1,1,1,2,256,256]{4,5,3,0,2,1:T(8,128)(2,1)S(1)}, u32[]{:S(2)}, u32[]{:S(2)}) collective-permute-start(bf16[1,1,1,2,256,256]{4,5,3,0,2,1:T(8,128)(2,1)S(1)} %get-tuple-element.10), channel_id=1, source_target_pairs={{0,16},{4,20},{8,24},{12,28},{16,0},{20,4},{24,8},{28,12},{1,17},{... | collective-permute-start | bytes 786440 | tf_op jit(solution)/shard_map/ppermute | solution.py:109
  83.5 13.1 %collective-permute-start.6 = (bf16[2,1,1,2,256,256]{4,5,3,0,2,1:T(8,128)(2,1)S(1)}, bf16[2,1,1,2,256,256]{4,5,3,0,2,1:T(8,128)(2,1)S(1)}, u32[]{:S(2)}, u32[]{:S(2)}) collective-permute-start(bf16[2,1,1,2,256,256]{4,5,3,0,2,1:T(8,128)(2,1)S(1)} %maximum_select_fusion.4), channel_id=1, source_target_pairs={{0,8},{4,12},{8,0},{12,4},{16,24},{20,28},{24,16},{28,20},{1,9},{5... | collective-permute-start | bytes 1572872 | tf_op jit(solution)/shard_map/ppermute | solution.py:109
  96.8 3.1 %copy-start.1 = (bf16[2,2,1,2,256,256]{4,5,3,0,2,1:T(8,128)(2,1)}, bf16[2,2,1,2,256,256]{4,5,3,0,2,1:T(8,128)(2,1)S(1)}, u32[]{:S(2)}) copy-start(bf16[2,2,1,2,256,256]{4,5,3,0,2,1:T(8,128)(2,1)S(1)} %maximum_select_fusion.2) | copy-start | bytes 3145732
  96.8 25.4 %collective-permute-start.7 = (bf16[2,2,1,2,256,256]{4,5,3,0,2,1:T(8,128)(2,1)S(1)}, bf16[2,2,1,2,256,256]{4,5,3,0,2,1:T(8,128)(2,1)}, u32[]{:S(2)}, u32[]{:S(2)}) collective-permute-start(bf16[2,2,1,2,256,256]{4,5,3,0,2,1:T(8,128)(2,1)S(1)} %maximum_select_fusion.2), channel_id=1, source_target_pairs={{0,4},{4,0},{8,12},{12,8},{16,20},{20,16},{24,28},{28,24},{1,5},{5... | collective-permute-start | bytes 3145736 | tf_op jit(solution)/shard_map/ppermute | solution.py:109
  131.4 1.6 %copy-start.3 = (bf16[256,1600]{1,0:T(8,128)(2,1)S(1)}, bf16[256,1600]{1,0:T(8,128)(2,1)}, u32[]{:S(2)}) copy-start(bf16[256,1600]{1,0:T(8,128)(2,1)} %copy-done.2) | copy-start | bytes 2457604
  141.1 13.2 %all-to-all-start.2 = ((bf16[32,16,200]{2,1,0:T(8,128)(2,1)}), bf16[32,16,200]{2,1,0:T(8,128)(2,1)S(1)}, u32[]{:S(2)}, u32[]{:S(2)}) async-start(bf16[32,16,200]{2,1,0:T(8,128)(2,1)} %pad_maximum_fusion.1), calls=%async_computation.2 | async-start | bytes 524288 | tf_op jit(solution)/shard_map/all_to_all | solution.py:192
  143.6 10.8 %copy-start.6 = (bf16[8,1600]{1,0:T(8,128)(2,1)S(1)}, bf16[8,1600]{1,0:T(8,128)(2,1)}, u32[]{:S(2)}) copy-start(bf16[8,1600]{1,0:T(8,128)(2,1)} %param.8) | copy-start | bytes 76804
  143.7 12.5 %copy-start.8 = (bf16[16,1600]{1,0:T(8,128)(2,1)S(1)}, bf16[16,1600]{1,0:T(8,128)(2,1)}, u32[]{:S(2)}) copy-start(bf16[16,1600]{1,0:T(8,128)(2,1)} %param.14) | copy-start | bytes 153604

commit v2 on v0

--- a/solution.py
+++ b/solution.py
@@ -1,6 +1,10 @@
+import functools
+
 import jax
 import jax.numpy as jnp
 from jax import lax
+from jax.experimental import pallas as pl
+from jax.experimental.pallas import tpu as pltpu
 from jax.sharding import PartitionSpec as P
 
 
@@ -15,7 +19,9 @@
     return (activated, derivative)
 
 
-def shards(patches, gain, expand_weight, project_weight, counts, positions, text, cotangent):
+def gather_weights_plan(
+    patches, gain, expand_weight, project_weight, counts, positions, text, cotangent
+):
     sections = lax.axis_size("section")
     slot_count = patches.shape[0]
     features = patches.shape[1]
@@ -93,6 +99,361 @@
     )
 
 
+def bit_steps(size):
+    steps = []
+    step = size // 2
+    while step >= 1:
+        steps.append(step)
+        step //= 2
+    return steps
+
+
+def swap(array, axis, step):
+    size = lax.axis_size(axis)
+    return lax.ppermute(array, axis, [(i, i ^ step) for i in range(size)])
+
+
+def masked_steps(index, steps):
+    mask = 0
+    for place, step in enumerate(steps):
+        mask = mask + ((index >> place) & 1) * step
+    return mask
+
+
+VMEM_SPEC = pl.BlockSpec(memory_space=pltpu.VMEM)
+SMEM_SPEC = pl.BlockSpec(memory_space=pltpu.SMEM)
+
+
+def log2(value):
+    return value.bit_length() - 1
+
+
+def landing(place_ref, count_ref, section, slots, capacity, length):
+    row = lax.broadcasted_iota(jnp.int32, (slots, length), 0)
+    column = lax.broadcasted_iota(jnp.int32, (slots, length), 1)
+    spot = jnp.full((slots, length), -1, jnp.int32)
+    for q in range(slots):
+        live = section * capacity + q % capacity < count_ref[0, q // capacity]
+        spot = jnp.where(row == q, jnp.where(live, place_ref[0, q], -1), spot)
+    return (spot == column).astype(jnp.float32)
+
+
+def pick_kernel(capacity, me_ref, count_ref, place_ref, patch_ref, cotangent_ref, pair_ref):
+    slots = patch_ref.shape[0]
+    chooser = landing(
+        place_ref, count_ref, me_ref[1], slots, capacity, cotangent_ref.shape[0]
+    ).astype(jnp.bfloat16)
+    picked = jnp.dot(chooser, cotangent_ref[...], preferred_element_type=jnp.float32)
+    pair_ref[0] = jnp.concatenate(
+        [patch_ref[...].astype(jnp.float32), picked], axis=0
+    ).astype(jnp.bfloat16)
+
+
+def repack_kernel(expand_ref, project_ref, out_ref):
+    units = out_ref.shape[3]
+    for d in range(out_ref.shape[0]):
+        out_ref[d, 0] = expand_ref[:, d * units : (d + 1) * units]
+        out_ref[d, 1] = project_ref[:, d * units : (d + 1) * units]
+
+
+def order_kernel(
+    sections, capacity, dp_steps, section_steps,
+    me_ref, near_ref, far_ref, gain_ref, normed_ref, grad_ref, extra_ref,
+):
+    rows = normed_ref.shape[0]
+    slots = sections * capacity
+    half = near_ref.shape[0] * near_ref.shape[1]
+    me_dp, me_section = me_ref[0], me_ref[1]
+    column = lax.broadcasted_iota(jnp.int32, (8, half), 1)
+    row = lax.broadcasted_iota(jnp.int32, (rows, half), 0)
+    kind = column & (2 * slots - 1)
+    slot = kind & (slots - 1)
+    inputs = grad = None
+    for side, ref in enumerate((near_ref, far_ref)):
+        block = (column >> log2(2 * slots)) + side * (half // (2 * slots))
+        source_dp = me_dp ^ masked_steps(block, dp_steps)
+        source_section = me_section ^ masked_steps(block >> len(dp_steps), section_steps)
+        patch_at = (source_dp * sections + source_section) * slots + slot
+        grad_at = (
+            (source_dp * sections + (slot >> log2(capacity))) * slots
+            + source_section * capacity
+            + (slot & (capacity - 1))
+        )
+        patch_at = jnp.where(kind < slots, patch_at, -1)[:1]
+        grad_at = jnp.where(kind >= slots, grad_at, -1)[:1]
+        values = ref[...].reshape(half, ref.shape[2])
+        chosen = (row == patch_at).astype(jnp.float32).astype(jnp.bfloat16)
+        found = jnp.dot(chosen, values, preferred_element_type=jnp.float32)
+        inputs = found if inputs is None else inputs + found
+        chosen = (row == grad_at).astype(jnp.float32).astype(jnp.bfloat16)
+        found = jnp.dot(chosen, values, preferred_element_type=jnp.float32)
+        grad = found if grad is None else grad + found
+    inv_rms = lax.rsqrt(jnp.mean(inputs * inputs, axis=-1, keepdims=True) + 1e-06)
+    normed_ref[...] = (inputs * inv_rms * gain_ref[...]).astype(jnp.bfloat16)
+    grad = grad.astype(jnp.bfloat16)
+    grad_ref[...] = grad
+    mine = lax.broadcasted_iota(jnp.int32, (slots, rows), 0)
+    every = lax.broadcasted_iota(jnp.int32, (slots, rows), 1)
+    coming_at = (
+        (me_dp * sections + (mine >> log2(capacity))) * slots
+        + me_section * capacity
+        + (mine & (capacity - 1))
+    )
+    own_at = (me_dp * sections + me_section) * slots + mine
+    coming = jnp.dot(
+        (every == coming_at).astype(jnp.float32).astype(jnp.bfloat16),
+        inputs.astype(jnp.bfloat16),
+        preferred_element_type=jnp.float32,
+    )
+    own = jnp.dot(
+        (every == own_at).astype(jnp.float32).astype(jnp.bfloat16),
+        grad,
+        preferred_element_type=jnp.float32,
+    )
+    extra_ref[...] = jnp.concatenate([coming, own], axis=0)
+
+
+def hidden_kernel(normed_ref, grad_ref, turned_ref, both_ref, expand_ref, project_ref):
+    part = turned_ref.shape[2]
+    for d in range(turned_ref.shape[0]):
+        expand_ref[d * part : (d + 1) * part, :] = turned_ref[d, 0]
+        project_ref[d * part : (d + 1) * part, :] = turned_ref[d, 1]
+    preact = jnp.dot(normed_ref[...], expand_ref[...], preferred_element_type=jnp.float32)
+    activated, derivative = gelu_pair(preact)
+    both_ref[0] = activated.astype(jnp.bfloat16)
+    grad_hidden = jnp.dot(grad_ref[...], project_ref[...], preferred_element_type=jnp.float32)
+    both_ref[1] = (grad_hidden * derivative).astype(jnp.bfloat16)
+
+
+def share_kernel(
+    sections, capacity, dp_steps, me_ref, near_ref, far_ref, expand_ref, project_ref, out_ref
+):
+    blocks, _, rows, units = near_ref.shape
+    devices, _, part = out_ref.shape
+    slots = sections * capacity
+    mixed = jnp.zeros((rows, part), jnp.float32)
+    grad_normed = jnp.zeros((rows, part), jnp.float32)
+    for side, ref in enumerate((near_ref, far_ref)):
+        for i in range(blocks):
+            source = me_ref[0] ^ masked_steps(side * blocks + i, dp_steps)
+            columns = pl.ds(pl.multiple_of(source * units, 128), units)
+            mixed += lax.dot_general(
+                ref[i, 0], project_ref[:, columns],
+                (((1,), (1,)), ((), ())), preferred_element_type=jnp.float32,
+            )
+            grad_normed += lax.dot_general(
+                ref[i, 1], expand_ref[:, columns],
+                (((1,), (1,)), ((), ())), preferred_element_type=jnp.float32,
+            )
+    row = lax.broadcasted_iota(jnp.int32, (rows, rows), 0)
+    column = lax.broadcasted_iota(jnp.int32, (rows, rows), 1)
+    inside = row & (slots - 1)
+    text_section = (row >> log2(slots)) & (sections - 1)
+    source_row = (
+        (row >> log2(slots * sections)) * (slots * sections)
+        + (inside >> log2(capacity)) * slots
+        + text_section * capacity
+        + (inside & (capacity - 1))
+    )
+    turn = (column == source_row).astype(jnp.float32).astype(jnp.bfloat16)
+    mixed = jnp.dot(turn, mixed.astype(jnp.bfloat16), preferred_element_type=jnp.float32)
+    out_ref[:, :slots, :] = mixed.reshape(devices, slots, part).astype(jnp.bfloat16)
+    out_ref[:, slots:, :] = grad_normed.reshape(devices, slots, part).astype(jnp.bfloat16)
+
+
+def weight_grad_kernel(me_ref, block_ref, normed_ref, grad_ref, *refs):
+    expand_ref, project_ref = refs[-2:]
+    contract = (((0,), (0,)), ((), ()))
+    expand_ref[...] = lax.dot_general(
+        normed_ref[...], block_ref[0, 1], contract, preferred_element_type=jnp.float32
+    ).astype(jnp.bfloat16)
+    project_ref[...] = lax.dot_general(
+        grad_ref[...], block_ref[0, 0], contract, preferred_element_type=jnp.float32
+    ).astype(jnp.bfloat16)
+
+
+def finish_kernel(
+    sections, capacity,
+    me_ref, count_ref, place_ref, tail_ref, extra_ref, patch_ref, text_ref, gain_ref,
+    embedded_ref, grad_rows_ref, sum_ref,
+):
+    devices, _, part = tail_ref.shape
+    slots = patch_ref.shape[0]
+    for d in range(devices // sections):
+        total = tail_ref[d * sections].astype(jnp.float32)
+        for s in range(1, sections):
+            total += tail_ref[d * sections + s].astype(jnp.float32)
+        sum_ref[:, d * part : (d + 1) * part] = total
+    mixed, grad_normed = sum_ref[:slots, :], sum_ref[slots:, :]
+    out_rows = (extra_ref[:slots, :] + mixed).astype(jnp.bfloat16)
+    length = text_ref.shape[0]
+    chooser = landing(place_ref, count_ref, me_ref[1], slots, capacity, length)
+    contract = (((0,), (0,)), ((), ()))
+    placed = lax.dot_general(
+        chooser.astype(jnp.bfloat16), out_rows, contract, preferred_element_type=jnp.float32
+    )
+    taken = lax.dot_general(
+        chooser.astype(jnp.bfloat16), jnp.ones((slots, 128), jnp.bfloat16),
+        contract, preferred_element_type=jnp.float32,
+    )[:, :1]
+    embedded_ref[...] = jnp.where(
+        taken > 0.5, placed, text_ref[...].astype(jnp.float32)
+    ).astype(jnp.bfloat16)
+    inputs = patch_ref[...].astype(jnp.float32)
+    inv_rms = lax.rsqrt(jnp.mean(inputs * inputs, axis=-1, keepdims=True) + 1e-06)
+    scaled_grad = grad_normed * gain_ref[...]
+    centred = jnp.mean(scaled_grad * inputs, axis=-1, keepdims=True)
+    grad_rows_ref[...] = (
+        extra_ref[slots:, :] + inv_rms * scaled_grad - inputs * (inv_rms**3 * centred)
+    ).astype(jnp.bfloat16)
+
+
+def weight_grads(me, blocks, first_index, dp_steps, normed, grad_all, width, before):
+    count, _, rows, units = blocks.shape
+    features = normed.shape[1]
+
+    def where_to(i, me_ref):
+        return me_ref[0] ^ masked_steps(first_index + i, dp_steps)
+
+    whole = pl.BlockSpec((rows, features), lambda i, me_ref: (0, 0))
+    in_specs = [
+        pl.BlockSpec((1, 2, rows, units), lambda i, me_ref: (i, 0, 0, 0)), whole, whole
+    ] + [pl.BlockSpec(memory_space=pl.ANY)] * len(before)
+    return pl.pallas_call(
+        weight_grad_kernel,
+        grid_spec=pltpu.PrefetchScalarGridSpec(
+            num_scalar_prefetch=1,
+            grid=(count,),
+            in_specs=in_specs,
+            out_specs=[
+                pl.BlockSpec((features, units), lambda i, me_ref: (0, where_to(i, me_ref)))
+            ] * 2,
+        ),
+        out_shape=[jax.ShapeDtypeStruct((features, width), jnp.bfloat16)] * 2,
+        input_output_aliases={4: 0, 5: 1} if before else {},
+        compiler_params=pltpu.CompilerParams(
+            dimension_semantics=("arbitrary",), vmem_limit_bytes=24 << 20
+        ),
+        cost_estimate=pl.CostEstimate(
+            flops=4 * count * rows * features * units,
+            bytes_accessed=4 * count * units * features + 4 * rows * features,
+            transcendentals=0,
+        ),
+    )(me, blocks, normed, grad_all, *before)
+
+
+def call(kernel, out_shape, smem, vmem, scratch=()):
+    single = not isinstance(out_shape, (list, tuple))
+    return pl.pallas_call(
+        kernel,
+        out_shape=out_shape,
+        in_specs=[SMEM_SPEC] * len(smem) + [VMEM_SPEC] * len(vmem),
+        out_specs=VMEM_SPEC if single else [VMEM_SPEC] * len(out_shape),
+        scratch_shapes=scratch,
+        compiler_params=pltpu.CompilerParams(vmem_limit_bytes=24 << 20),
+    )(*smem, *vmem)
+
+
+def move_rows_plan(
+    patches, gain, expand_weight, project_weight, counts, positions, text, cotangent
+):
+    sections = lax.axis_size("section")
+    replicas = lax.axis_size("dp")
+    devices = sections * replicas
+    slots, features = patches.shape
+    part, width = expand_weight.shape
+    units = width // replicas
+    capacity = slots // sections
+    rows = devices * slots
+    dp_steps, section_steps = bit_steps(replicas), bit_steps(sections)
+    me = jnp.stack([lax.axis_index("dp"), lax.axis_index("section")]).astype(jnp.int32)
+    gain = gain.reshape(1, features)
+    project_turned = project_weight.T
+    kept, wide = jnp.bfloat16, jnp.float32
+    shape = jax.ShapeDtypeStruct
+
+    stacked = call(
+        repack_kernel,
+        shape((replicas, 2, part, units), kept),
+        (), (expand_weight, project_turned),
+    )
+    turned = lax.all_to_all(stacked, "dp", split_axis=0, concat_axis=0, tiled=True)
+
+    held = call(
+        functools.partial(pick_kernel, capacity),
+        shape((1, 2 * slots, features), kept),
+        (me, counts, positions), (patches, cotangent),
+    )
+    for axis, step in [("dp", s) for s in dp_steps] + [("section", s) for s in section_steps]:
+        got = swap(held, axis, step)
+        if held.shape[0] < devices // 2:
+            held = jnp.concatenate([held, got], axis=0)
+    normed, grad_all, extra = call(
+        functools.partial(order_kernel, sections, capacity, dp_steps, section_steps),
+        [shape((rows, features), kept), shape((rows, features), kept), shape((2 * slots, features), wide)],
+        (me,), (held, got, gain),
+    )
+
+    both = call(
+        hidden_kernel,
+        shape((2, rows, units), kept),
+        (), (normed, grad_all, turned),
+        [pltpu.VMEM((features, units), kept)] * 2,
+    )
+
+    near = both[None]
+    for step in dp_steps:
+        far = swap(near, "dp", step)
+        if near.shape[0] < replicas // 2:
+            near = jnp.concatenate([near, far], axis=0)
+
+    grads = weight_grads(me, near, 0, dp_steps, normed, grad_all, width, ())
+    tail = call(
+        functools.partial(share_kernel, sections, capacity, dp_steps),
+        shape((devices, 2 * slots, part), kept),
+        (me,), (near, far, expand_weight, project_turned),
+    )
+    tail = lax.all_to_all(
+        tail, ("dp", "section"), split_axis=0, concat_axis=0, tiled=True
+    )
+    expand_grad, project_grad = weight_grads(
+        me, far, replicas // 2, dp_steps, normed, grad_all, width, grads
+    )
+    embedded, grad_rows = call(
+        functools.partial(finish_kernel, sections, capacity),
+        [shape(text.shape, kept), shape(patches.shape, kept)],
+        (me, counts, positions), (tail, extra, patches, text, gain),
+        [pltpu.VMEM((2 * slots, features), wide)],
+    )
+    return (embedded, grad_rows, expand_grad, project_grad.T)
+
+
+def power_of_two(value):
+    return value > 0 and value & (value - 1) == 0
+
+
+def shards(patches, gain, expand_weight, project_weight, counts, positions, text, cotangent):
+    replicas, sections = lax.axis_size("dp"), lax.axis_size("section")
+    slots, features = patches.shape
+    width = expand_weight.shape[1]
+    rows = replicas * sections * slots
+    fits = rows * (features + width) <= features * width
+    even = (
+        all(power_of_two(n) for n in (replicas, sections, slots))
+        and replicas > 1
+        and sections > 1
+        and slots % 8 == 0
+        and width % (128 * replicas) == 0
+    )
+    if fits and even:
+        plan = move_rows_plan
+    else:
+        plan = gather_weights_plan
+    return plan(
+        patches, gain, expand_weight, project_weight, counts, positions, text, cotangent
+    )
+
+
 def solution(mesh):
     return jax.shard_map(
         shards,

time: 687 us -> 155 us (0.23)
  waiting for transfers between devices: 611 us -> 103 us
  starting transfers between devices: 0.16 us -> 24 us
  matrix products: 23.2 us -> 0 us
  blocking collectives: 18.2 us -> 0 us
  Pallas kernels: 0 us -> 18.1 us
  between operations: 14.5 us -> 0.78 us
    psum x1 -> x0, waiting for transfers between devices: 404 us -> none  [shards(): lax.psum(expand_local.astype(jnp.bfloat16), 'dp').astype(jnp.float32)]
    all_gather x2 -> x0, waiting for transfers between devices: 183 us -> none  [the longest x1 93.5 us: shards(): lax.all_gather(project_weight, 'dp', axis=1, tiled=True)]
    ppermute x0 -> x8, waiting for transfers between devices: none -> 103 us  [swap(): return lax.ppermute(array, axis, [(i, i ^ step) for i in range(size)])]
    unnamed x5 -> x0, waiting for transfers between devices: 24.5 us -> none
    dot_general x6 -> x0, matrix products: 23.2 us -> none  [the longest x1 5.68 us: shards(): jnp.dot(row_block, project_full, preferred_element_type=jnp.float32)]
    pallas_call x0 -> x8, Pallas kernels: none -> 18.1 us  [the longest x2 9.67 us: weight_grads(): pl.pallas_call(weight_grad_kernel, grid_spec=pltpu.PrefetchScalarGridSpec...]
    all_to_all x0 -> x2, starting transfers between devices: none -> 12.4 us  [the longest x1 7.28 us: move_rows_plan(): lax.all_to_all(stacked, 'dp', split_axis=0, concat_axis=0, tiled=True)]
    all_gather x2 -> x0, blocking collectives: 12 us -> none  [the longest x1 6.39 us: shards(): collected = lax.all_gather(picked, 'section', axis=0, tiled=True)]
  transfers between devices with their start and end apart: 4 -> 10, of which waited for: 4 -> 8; matrix products, arithmetic and copies ran while one was open for 3% -> 0% of each run, Pallas kernels for 0% -> 8%
where the time goes in v2:
time: 155 us; the launch traced here: 154 us
  waiting for transfers between devices  103 us (66%)
  starting transfers between devices  24 us (15%)
  Pallas kernels  18.1 us (12%)
  local copies, waits for them, and re-layouts  7.93 us (5%)
    ppermute x8, waiting for transfers between devices, swap(): return lax.ppermute(array, axis, [(i, i ^ step) for i in range(size)])  103 us
    ppermute x8, starting transfers between devices, swap(): return lax.ppermute(array, axis, [(i, i ^ step) for i in range(size)])  11.6 us
    pallas_call x2, Pallas kernels, weight_grads(): pl.pallas_call(weight_grad_kernel, grid_spec=pltpu.PrefetchScalarGridSpec...  9.67 us
    pallas_call x6, Pallas kernels, call(): pl.pallas_call(kernel, out_shape=out_shape, in_specs=[SMEM_SPEC] * len(sm...  8.39 us
    unnamed x30, local copies, waits for them, and re-layouts  7.89 us
    all_to_all x1, starting transfers between devices, move_rows_plan(): lax.all_to_all(stacked, 'dp', split_axis=0, concat_axis=0, tiled=True)  7.28 us
    all_to_all x1, starting transfers between devices, move_rows_plan(): lax.all_to_all(tail, ('dp', 'section'), split_axis=0, concat_axis=0, tile...  5.09 us
  transfers between devices with their start and end apart: 10, of which 8 were waited for; matrix products, arithmetic and copies ran while one was open for 0% of the time, Pallas kernels for 8%

profile of v2, /device:TPU:0, one launch (start us, length us, event | category | flops | bytes accessed | tf_op | source)
XLA Modules:
  0.0 154.3 jit_solution(2525907602308328711)
XLA Ops:
  0.6 0.0 copy-start.11
  0.6 0.0 copy-start.10
  0.7 0.0 copy-start.3
  0.7 1.1 copy-done.3
  1.8 1.1 copy-done.5
  3.0 1.3 shard_map.113
  4.2 7.3 %all-to-all-start = ((bf16[8,2,200,256]{3,2,1,0:T(8,128)(2,1)}), bf16[8,2,200,256]{3,2,1,0:T(8,128)(2,1)S(1)}, u32[]{:S(2)}, u32[]{:S(2)}) async-start(bf16[8,2,200,256]{3,2,1,0:T(8,128)(2,1)} %shard_map.113), calls=%async_computation | async-start | bytes 3276800 | tf_op jit(solution)/shard_map/all_to_all | solution.py:380
  11.5 0.1 pad_add_fusion.me_ref
  11.6 0.0 copy-done.11
  11.6 0.0 copy-done.10
  11.6 0.0 copy-done.7
  11.6 0.0 copy-done.9
  11.6 0.7 shard_map.111
  12.3 3.0 %collective-permute-start = (bf16[1,16,1600]{2,1,0:T(8,128)(2,1)S(1)}, bf16[1,16,1600]{2,1,0:T(8,128)(2,1)S(1)}, u32[]{:S(2)}, u32[]{:S(2)}) collective-permute-start(bf16[1,16,1600]{2,1,0:T(8,128)(2,1)S(1)} %shard_map.111), channel_id=1, source_target_pairs={{0,16},{4,20},{8,24},{12,28},{16,0},{20,4},{24,8},{28,12},{1,17},{... | collective-permute-start | bytes 153608 | tf_op jit(solution)/shard_map/ppermute | solution.py:113
  15.3 36.9 %collective-permute-done = bf16[1,16,1600]{2,1,0:T(8,128)(2,1)S(1)} collective-permute-done((bf16[1,16,1600]{2,1,0:T(8,128)(2,1)S(1)}, bf16[1,16,1600]{2,1,0:T(8,128)(2,1)S(1)}, u32[]{:S(2)}, u32[]{:S(2)}) %collective-permute-start) | collective-permute-done | bytes 51232 | tf_op jit(solution)/shard_map/ppermute | solution.py:113
  52.2 0.1 collective-permute-start.1
  52.3 4.7 %collective-permute-done.1 = bf16[2,16,1600]{2,1,0:T(8,128)(2,1)S(1)} collective-permute-done((bf16[2,16,1600]{2,1,0:T(8,128)(2,1)S(1)}, bf16[2,16,1600]{2,1,0:T(8,128)(2,1)S(1)}, u32[]{:S(2)}, u32[]{:S(2)}) %collective-permute-start.1) | collective-permute-done | bytes 102432 | tf_op jit(solution)/shard_map/ppermute | solution.py:113
  57.0 1.5 collective-permute-start.2
  58.6 4.4 %collective-permute-done.2 = bf16[4,16,1600]{2,1,0:T(8,128)(2,1)S(1)} collective-permute-done((bf16[4,16,1600]{2,1,0:T(8,128)(2,1)S(1)}, bf16[4,16,1600]{2,1,0:T(8,128)(2,1)S(1)}, u32[]{:S(2)}, u32[]{:S(2)}) %collective-permute-start.2) | collective-permute-done | bytes 204832 | tf_op jit(solution)/shard_map/ppermute | solution.py:113
  63.0 0.1 pad_maximum_fusion.2
  63.0 1.6 %collective-permute-start.3 = (bf16[8,16,1600]{2,1,0:T(8,128)(2,1)S(1)}, bf16[8,16,1600]{2,1,0:T(8,128)(2,1)S(1)}, u32[]{:S(2)}, u32[]{:S(2)}) collective-permute-start(bf16[8,16,1600]{2,1,0:T(8,128)(2,1)S(1)} %pad_maximum_fusion.2), channel_id=1, source_target_pairs={{0,2},{1,3},{2,0},{3,1},{4,6},{5,7},{6,4},{7,5},{8,10},{9,11},{10,... | collective-permute-start | bytes 1228808 | tf_op jit(solution)/shard_map/ppermute | solution.py:113
  64.7 6.7 %collective-permute-done.3 = bf16[8,16,1600]{2,1,0:T(8,128)(2,1)S(1)} collective-permute-done((bf16[8,16,1600]{2,1,0:T(8,128)(2,1)S(1)}, bf16[8,16,1600]{2,1,0:T(8,128)(2,1)S(1)}, u32[]{:S(2)}, u32[]{:S(2)}) %collective-permute-start.3) | collective-permute-done | bytes 409632 | tf_op jit(solution)/shard_map/ppermute | solution.py:113
  71.4 0.1 collective-permute-start.4
  71.5 2.3 %collective-permute-done.4.far_ref = bf16[16,16,1600]{2,1,0:T(8,128)(2,1)S(1)} collective-permute-done((bf16[16,16,1600]{2,1,0:T(8,128)(2,1)S(1)}, bf16[16,16,1600]{2,1,0:T(8,128)(2,1)S(1)}, u32[]{:S(2)}, u32[]{:S(2)}) %collective-permute-start.4) | collective-permute-done | bytes 819232 | tf_op jit(solution)/shard_map/ppermute | solution.py:113
  73.8 2.0 %shard_map.112 = (bf16[256,1600]{1,0:T(8,128)(2,1)S(1)}, bf16[256,1600]{1,0:T(8,128)(2,1)S(1)}, f32[16,1600]{1,0:T(8,128)S(1)}) custom-call(s32[2]{0:T(128)S(1)} %pad_add_fusion.me_ref, bf16[16,16,1600]{2,1,0:T(8,128)(2,1)S(1)} %constant_dynamic-update-slice_fusion.near_ref, bf16[16,16,1600]{2,1,0:T(8,128)(2,1)S(1)} %collective-permute-done.4.far_ref, ...), custom_call_target="tpu_custom_call" | custom-call | tf_op jit(solution)/shard_map/pallas_call | solution.py:347
  75.9 0.9 copy-done
  76.8 0.0 all-to-all-done.turned_ref
  76.8 1.2 copy-done.1
  77.9 0.8 shard_map.114
  78.7 4.1 %collective-permute-start.5 = (bf16[1,2,256,256]{3,2,1,0:T(8,128)(2,1)S(1)}, bf16[1,2,256,256]{3,2,1,0:T(8,128)(2,1)S(1)}, u32[]{:S(2)}, u32[]{:S(2)}) collective-permute-start(bf16[1,2,256,256]{3,2,1,0:T(8,128)(2,1)S(1)} %bitcast.7), channel_id=1, source_target_pairs={{0,16},{4,20},{8,24},{12,28},{16,0},{20,4},{24,8},{28,12},{1,17},{... | collective-permute-start | bytes 786440 | tf_op jit(solution)/shard_map/ppermute | solution.py:113
  82.8 12.2 %collective-permute-done.5 = bf16[1,2,256,256]{3,2,1,0:T(8,128)(2,1)S(1)} collective-permute-done((bf16[1,2,256,256]{3,2,1,0:T(8,128)(2,1)S(1)}, bf16[1,2,256,256]{3,2,1,0:T(8,128)(2,1)S(1)}, u32[]{:S(2)}, u32[]{:S(2)}) %collective-permute-start.5) | collective-permute-done | bytes 262176 | tf_op jit(solution)/shard_map/ppermute | solution.py:113
  95.0 0.1 pad_maximum_fusion.1
  95.1 0.5 collective-permute-start.6
  95.6 13.0 %collective-permute-done.6 = bf16[2,2,256,256]{3,2,1,0:T(8,128)(2,1)S(1)} collective-permute-done((bf16[2,2,256,256]{3,2,1,0:T(8,128)(2,1)S(1)}, bf16[2,2,256,256]{3,2,1,0:T(8,128)(2,1)S(1)}, u32[]{:S(2)}, u32[]{:S(2)}) %collective-permute-start.6) | collective-permute-done | bytes 524320 | tf_op jit(solution)/shard_map/ppermute | solution.py:113
  108.5 0.1 pad_maximum_fusion.near_ref.block_ref
  108.6 0.8 collective-permute-start.7
  109.4 23.0 %collective-permute-done.7.far_ref.block_ref = bf16[4,2,256,256]{3,2,1,0:T(8,128)(2,1)S(1)} collective-permute-done((bf16[4,2,256,256]{3,2,1,0:T(8,128)(2,1)S(1)}, bf16[4,2,256,256]{3,2,1,0:T(8,128)(2,1)S(1)}, u32[]{:S(2)}, u32[]{:S(2)}) %collective-permute-start.7) | collective-permute-done | bytes 1048608 | tf_op jit(solution)/shard_map/ppermute | solution.py:113
  132.5 1.1 copy-done.4
  133.6 1.1 copy-done.6
  134.7 2.2 %shard_map.115 = bf16[32,16,200]{2,1,0:T(8,128)(2,1)} custom-call(s32[2]{0:T(128)S(1)} %pad_add_fusion.me_ref, bf16[4,2,256,256]{3,2,1,0:T(8,128)(2,1)S(1)} %pad_maximum_fusion.near_ref.block_ref, bf16[4,2,256,256]{3,2,1,0:T(8,128)(2,1)S(1)} %collective-permute-done.7.far_ref.block_ref, bf16[200,2048]{1,0:T(8,128)(2,1)S(1)} %copy-done.4, ...), custom_call_target="tpu_custom_call" | custom-call | tf_op jit(solution)/shard_map/pallas_call | solution.py:347
  136.9 5.1 %all-to-all-start.1 = ((bf16[32,16,200]{2,1,0:T(8,128)(2,1)}), bf16[32,16,200]{2,1,0:T(8,128)(2,1)S(1)}, u32[]{:S(2)}, u32[]{:S(2)}) async-start(bf16[32,16,200]{2,1,0:T(8,128)(2,1)} %shard_map.115), calls=%async_computation.1 | async-start | bytes 524288 | tf_op jit(solution)/shard_map/all_to_all | solution.py:416
  142.0 0.0 copy-start.2
  142.0 1.1 copy-done.2
  143.2 4.8 %shard_map.117 = (bf16[1600,2048]{1,0:T(8,128)(2,1)}, bf16[1600,2048]{1,0:T(8,128)(2,1)}) custom-call(s32[2]{0:T(128)S(1)} %pad_add_fusion.me_ref, bf16[4,2,256,256]{3,2,1,0:T(8,128)(2,1)S(1)} %pad_maximum_fusion.near_ref.block_ref, bf16[256,1600]{1,0:T(8,128)(2,1)S(1)} %get-tuple-element.13.normed_ref, bf16[256,1600]{1,0:T(8,128)(2,1)S(1)} %copy-done.2), custom_call_target="tpu_custom_call" | custom-call | flops 1677721600 | bytes 8192000 | tf_op jit(solution)/shard_map/pallas_call | solution.py:322
  148.0 4.8 %shard_map.118 = (bf16[1600,2048]{1,0:T(8,128)(2,1)}, bf16[1600,2048]{1,0:T(8,128)(2,1)}) custom-call(s32[2]{0:T(128)S(1)} %pad_add_fusion.me_ref, bf16[4,2,256,256]{3,2,1,0:T(8,128)(2,1)S(1)} %collective-permute-done.7.far_ref.block_ref, bf16[256,1600]{1,0:T(8,128)(2,1)S(1)} %get-tuple-element.13.normed_ref, ...), custom_call_target="tpu_custom_call", output_to_operand_aliasing={{0}: (4, {}), {1}: (5, {})} | custom-call | flops 1677721600 | bytes 8192000 | tf_op jit(solution)/shard_map/pallas_call | solution.py:322
  152.8 0.0 all-to-all-done.1.tail_ref
  152.8 0.0 copy-done.8
  152.8 1.5 shard_map.116
  (18 shorter events, 0.2 us)
Async XLA Ops:
  0.6 11.0 %copy-start.11 = (s32[1,8]{1,0:T(1,128)S(1)}, s32[1,8]{1,0:T(1,128)}, u32[]{:S(2)}) copy-start(s32[1,8]{1,0:T(1,128)} %place_ref.3) | copy-start | bytes 100
  0.6 11.0 %copy-start.10 = (s32[1,4]{1,0:T(1,128)S(1)}, s32[1,4]{1,0:T(1,128)}, u32[]{:S(2)}) copy-start(s32[1,4]{1,0:T(1,128)} %count_ref.3) | copy-start | bytes 52
  0.7 1.2 copy-start.3
  1.8 1.1 copy-start.5
  3.0 8.7 %copy-start.7 = (bf16[8,1600]{1,0:T(8,128)(2,1)S(1)}, bf16[8,1600]{1,0:T(8,128)(2,1)}, u32[]{:S(2)}) copy-start(bf16[8,1600]{1,0:T(8,128)(2,1)} %patch_ref.3) | copy-start | bytes 76804
  3.0 8.7 %copy-start.9 = (bf16[16,1600]{1,0:T(8,128)(2,1)S(1)}, bf16[16,1600]{1,0:T(8,128)(2,1)}, u32[]{:S(2)}) copy-start(bf16[16,1600]{1,0:T(8,128)(2,1)} %cotangent_ref.1) | copy-start | bytes 153604
  3.0 68.5 %copy-start.12 = (f32[1600]{0:T(1024)S(1)}, f32[1600]{0:T(1024)}, u32[]{:S(2)}) copy-start(f32[1600]{0:T(1024)} %param.9) | copy-start | bytes 19204
  4.2 72.5 %all-to-all-start = ((bf16[8,2,200,256]{3,2,1,0:T(8,128)(2,1)}), bf16[8,2,200,256]{3,2,1,0:T(8,128)(2,1)S(1)}, u32[]{:S(2)}, u32[]{:S(2)}) async-start(bf16[8,2,200,256]{3,2,1,0:T(8,128)(2,1)} %shard_map.113), calls=%async_computation | async-start | bytes 3276800 | tf_op jit(solution)/shard_map/all_to_all | solution.py:380
  12.3 39.9 %collective-permute-start = (bf16[1,16,1600]{2,1,0:T(8,128)(2,1)S(1)}, bf16[1,16,1600]{2,1,0:T(8,128)(2,1)S(1)}, u32[]{:S(2)}, u32[]{:S(2)}) collective-permute-start(bf16[1,16,1600]{2,1,0:T(8,128)(2,1)S(1)} %shard_map.111), channel_id=1, source_target_pairs={{0,16},{4,20},{8,24},{12,28},{16,0},{20,4},{24,8},{28,12},{1,17},{... | collective-permute-start | bytes 153608 | tf_op jit(solution)/shard_map/ppermute | solution.py:113
  52.2 4.8 %collective-permute-start.1 = (bf16[2,16,1600]{2,1,0:T(8,128)(2,1)S(1)}, bf16[2,16,1600]{2,1,0:T(8,128)(2,1)S(1)}, u32[]{:S(2)}, u32[]{:S(2)}) collective-permute-start(bf16[2,16,1600]{2,1,0:T(8,128)(2,1)S(1)} %pad_maximum_fusion.4), channel_id=1, source_target_pairs={{0,8},{4,12},{8,0},{12,4},{16,24},{20,28},{24,16},{28,20},{1,9},{5... | collective-permute-start | bytes 307208 | tf_op jit(solution)/shard_map/ppermute | solution.py:113
  57.0 5.9 %collective-permute-start.2 = (bf16[4,16,1600]{2,1,0:T(8,128)(2,1)S(1)}, bf16[4,16,1600]{2,1,0:T(8,128)(2,1)S(1)}, u32[]{:S(2)}, u32[]{:S(2)}) collective-permute-start(bf16[4,16,1600]{2,1,0:T(8,128)(2,1)S(1)} %pad_maximum_fusion.3), channel_id=1, source_target_pairs={{0,4},{4,0},{8,12},{12,8},{16,20},{20,16},{24,28},{28,24},{1,5},{5... | collective-permute-start | bytes 614408 | tf_op jit(solution)/shard_map/ppermute | solution.py:113
  63.0 8.3 %collective-permute-start.3 = (bf16[8,16,1600]{2,1,0:T(8,128)(2,1)S(1)}, bf16[8,16,1600]{2,1,0:T(8,128)(2,1)S(1)}, u32[]{:S(2)}, u32[]{:S(2)}) collective-permute-start(bf16[8,16,1600]{2,1,0:T(8,128)(2,1)S(1)} %pad_maximum_fusion.2), channel_id=1, source_target_pairs={{0,2},{1,3},{2,0},{3,1},{4,6},{5,7},{6,4},{7,5},{8,10},{9,11},{10,... | collective-permute-start | bytes 1228808 | tf_op jit(solution)/shard_map/ppermute | solution.py:113
  71.4 2.4 %collective-permute-start.4 = (bf16[16,16,1600]{2,1,0:T(8,128)(2,1)S(1)}, bf16[16,16,1600]{2,1,0:T(8,128)(2,1)S(1)}, u32[]{:S(2)}, u32[]{:S(2)}) collective-permute-start(bf16[16,16,1600]{2,1,0:T(8,128)(2,1)S(1)} %constant_dynamic-update-slice_fusion.near_ref), channel_id=1, source_target_pairs={{0,1},{1,0},{2,3},{3,2},{4,5},{5,4},{6,7},{7,6},{8,9},{9,8},{10,11... | collective-permute-start | bytes 2457608 | tf_op jit(solution)/shard_map/ppermute | solution.py:113
  75.9 0.9 copy-start
  76.8 1.2 copy-start.1
  78.7 16.3 %collective-permute-start.5 = (bf16[1,2,256,256]{3,2,1,0:T(8,128)(2,1)S(1)}, bf16[1,2,256,256]{3,2,1,0:T(8,128)(2,1)S(1)}, u32[]{:S(2)}, u32[]{:S(2)}) collective-permute-start(bf16[1,2,256,256]{3,2,1,0:T(8,128)(2,1)S(1)} %bitcast.7), channel_id=1, source_target_pairs={{0,16},{4,20},{8,24},{12,28},{16,0},{20,4},{24,8},{28,12},{1,17},{... | collective-permute-start | bytes 786440 | tf_op jit(solution)/shard_map/ppermute | solution.py:113
  95.1 13.5 %collective-permute-start.6 = (bf16[2,2,256,256]{3,2,1,0:T(8,128)(2,1)S(1)}, bf16[2,2,256,256]{3,2,1,0:T(8,128)(2,1)S(1)}, u32[]{:S(2)}, u32[]{:S(2)}) collective-permute-start(bf16[2,2,256,256]{3,2,1,0:T(8,128)(2,1)S(1)} %pad_maximum_fusion.1), channel_id=1, source_target_pairs={{0,8},{4,12},{8,0},{12,4},{16,24},{20,28},{24,16},{28,20},{1,9},{5... | collective-permute-start | bytes 1572872 | tf_op jit(solution)/shard_map/ppermute | solution.py:113
  108.6 23.8 %collective-permute-start.7 = (bf16[4,2,256,256]{3,2,1,0:T(8,128)(2,1)S(1)}, bf16[4,2,256,256]{3,2,1,0:T(8,128)(2,1)S(1)}, u32[]{:S(2)}, u32[]{:S(2)}) collective-permute-start(bf16[4,2,256,256]{3,2,1,0:T(8,128)(2,1)S(1)} %pad_maximum_fusion.near_ref.block_ref), channel_id=1, source_target_pairs={{0,4},{4,0},{8,12},{12,8},{16,20},{20,16},{24,28},{28,24},{1,5},{5... | collective-permute-start | bytes 3145736 | tf_op jit(solution)/shard_map/ppermute | solution.py:113
  132.5 1.1 copy-start.4
  133.6 1.1 copy-start.6
  136.9 15.9 %all-to-all-start.1 = ((bf16[32,16,200]{2,1,0:T(8,128)(2,1)}), bf16[32,16,200]{2,1,0:T(8,128)(2,1)S(1)}, u32[]{:S(2)}, u32[]{:S(2)}) async-start(bf16[32,16,200]{2,1,0:T(8,128)(2,1)} %shard_map.115), calls=%async_computation.1 | async-start | bytes 524288 | tf_op jit(solution)/shard_map/all_to_all | solution.py:416
  142.0 1.2 copy-start.2
  148.0 4.8 %copy-start.8 = (bf16[16,1600]{1,0:T(8,128)(2,1)S(1)}, bf16[16,1600]{1,0:T(8,128)(2,1)}, u32[]{:S(2)}) copy-start(bf16[16,1600]{1,0:T(8,128)(2,1)} %text_ref.1) | copy-start | bytes 153604

commit v3 on v2

--- a/solution.py
+++ b/solution.py
@@ -213,38 +213,43 @@
     extra_ref[...] = jnp.concatenate([coming, own], axis=0)
 
 
-def hidden_kernel(normed_ref, grad_ref, turned_ref, both_ref, expand_ref, project_ref):
+def hidden_kernel(
+    normed_ref, grad_ref, turned_ref, hidden_ref, pre_ref, expand_ref, project_ref
+):
     part = turned_ref.shape[2]
     for d in range(turned_ref.shape[0]):
         expand_ref[d * part : (d + 1) * part, :] = turned_ref[d, 0]
         project_ref[d * part : (d + 1) * part, :] = turned_ref[d, 1]
     preact = jnp.dot(normed_ref[...], expand_ref[...], preferred_element_type=jnp.float32)
     activated, derivative = gelu_pair(preact)
-    both_ref[0] = activated.astype(jnp.bfloat16)
+    hidden_ref[0] = activated.astype(jnp.bfloat16)
     grad_hidden = jnp.dot(grad_ref[...], project_ref[...], preferred_element_type=jnp.float32)
-    both_ref[1] = (grad_hidden * derivative).astype(jnp.bfloat16)
+    pre_ref[0] = (grad_hidden * derivative).astype(jnp.bfloat16)
 
 
 def share_kernel(
-    sections, capacity, dp_steps, me_ref, near_ref, far_ref, expand_ref, project_ref, out_ref
-):
-    blocks, _, rows, units = near_ref.shape
+    sections, capacity, hidden_steps, pre_steps,
+    me_ref, hidden_near_ref, hidden_far_ref, pre_near_ref, pre_far_ref,
+    expand_ref, project_ref, out_ref,
+):
+    blocks, rows, units = hidden_near_ref.shape
     devices, _, part = out_ref.shape
     slots = sections * capacity
-    mixed = jnp.zeros((rows, part), jnp.float32)
-    grad_normed = jnp.zeros((rows, part), jnp.float32)
-    for side, ref in enumerate((near_ref, far_ref)):
-        for i in range(blocks):
-            source = me_ref[0] ^ masked_steps(side * blocks + i, dp_steps)
-            columns = pl.ds(pl.multiple_of(source * units, 128), units)
-            mixed += lax.dot_general(
-                ref[i, 0], project_ref[:, columns],
-                (((1,), (1,)), ((), ())), preferred_element_type=jnp.float32,
-            )
-            grad_normed += lax.dot_general(
-                ref[i, 1], expand_ref[:, columns],
-                (((1,), (1,)), ((), ())), preferred_element_type=jnp.float32,
-            )
+
+    def product(near_ref, far_ref, weight_ref, steps):
+        total = jnp.zeros((rows, part), jnp.float32)
+        for side, ref in enumerate((near_ref, far_ref)):
+            for i in range(blocks):
+                source = me_ref[0] ^ masked_steps(side * blocks + i, steps)
+                columns = pl.ds(pl.multiple_of(source * units, 128), units)
+                total += lax.dot_general(
+                    ref[i], weight_ref[:, columns],
+                    (((1,), (1,)), ((), ())), preferred_element_type=jnp.float32,
+                )
+        return total
+
+    mixed = product(hidden_near_ref, hidden_far_ref, project_ref, hidden_steps)
+    grad_normed = product(pre_near_ref, pre_far_ref, expand_ref, pre_steps)
     row = lax.broadcasted_iota(jnp.int32, (rows, rows), 0)
     column = lax.broadcasted_iota(jnp.int32, (rows, rows), 1)
     inside = row & (slots - 1)
@@ -261,14 +266,14 @@
     out_ref[:, slots:, :] = grad_normed.reshape(devices, slots, part).astype(jnp.bfloat16)
 
 
-def weight_grad_kernel(me_ref, block_ref, normed_ref, grad_ref, *refs):
+def weight_grad_kernel(me_ref, hidden_ref, pre_ref, normed_ref, grad_ref, *refs):
     expand_ref, project_ref = refs[-2:]
     contract = (((0,), (0,)), ((), ()))
     expand_ref[...] = lax.dot_general(
-        normed_ref[...], block_ref[0, 1], contract, preferred_element_type=jnp.float32
+        normed_ref[...], pre_ref[0], contract, preferred_element_type=jnp.float32
     ).astype(jnp.bfloat16)
     project_ref[...] = lax.dot_general(
-        grad_ref[...], block_ref[0, 0], contract, preferred_element_type=jnp.float32
+        grad_ref[...], hidden_ref[0], contract, preferred_element_type=jnp.float32
     ).astype(jnp.bfloat16)
 
 
@@ -308,29 +313,31 @@
     ).astype(jnp.bfloat16)
 
 
-def weight_grads(me, blocks, first_index, dp_steps, normed, grad_all, width, before):
-    count, _, rows, units = blocks.shape
+def weight_grads(
+    me, hidden, pre, first_index, hidden_steps, pre_steps, normed, grad_all, width, before
+):
+    count, rows, units = hidden.shape
     features = normed.shape[1]
 
-    def where_to(i, me_ref):
-        return me_ref[0] ^ masked_steps(first_index + i, dp_steps)
+    def column(steps):
+        return lambda i, me_ref: (0, me_ref[0] ^ masked_steps(first_index + i, steps))
 
     whole = pl.BlockSpec((rows, features), lambda i, me_ref: (0, 0))
-    in_specs = [
-        pl.BlockSpec((1, 2, rows, units), lambda i, me_ref: (i, 0, 0, 0)), whole, whole
-    ] + [pl.BlockSpec(memory_space=pl.ANY)] * len(before)
+    block = pl.BlockSpec((1, rows, units), lambda i, me_ref: (i, 0, 0))
     return pl.pallas_call(
         weight_grad_kernel,
         grid_spec=pltpu.PrefetchScalarGridSpec(
             num_scalar_prefetch=1,
             grid=(count,),
-            in_specs=in_specs,
+            in_specs=[block, block, whole, whole]
+            + [pl.BlockSpec(memory_space=pl.ANY)] * len(before),
             out_specs=[
-                pl.BlockSpec((features, units), lambda i, me_ref: (0, where_to(i, me_ref)))
-            ] * 2,
+                pl.BlockSpec((features, units), column(pre_steps)),
+                pl.BlockSpec((features, units), column(hidden_steps)),
+            ],
         ),
         out_shape=[jax.ShapeDtypeStruct((features, width), jnp.bfloat16)] * 2,
-        input_output_aliases={4: 0, 5: 1} if before else {},
+        input_output_aliases={5: 0, 6: 1} if before else {},
         compiler_params=pltpu.CompilerParams(
             dimension_semantics=("arbitrary",), vmem_limit_bytes=24 << 20
         ),
@@ -339,7 +346,7 @@
             bytes_accessed=4 * count * units * features + 4 * rows * features,
             transcendentals=0,
         ),
-    )(me, blocks, normed, grad_all, *before)
+    )(me, hidden, pre, normed, grad_all, *before)
 
 
 def call(kernel, out_shape, smem, vmem, scratch=()):
@@ -384,7 +391,8 @@
         shape((1, 2 * slots, features), kept),
         (me, counts, positions), (patches, cotangent),
     )
-    for axis, step in [("dp", s) for s in dp_steps] + [("section", s) for s in section_steps]:
+    exchanges = [("dp", step) for step in dp_steps] + [("section", step) for step in section_steps]
+    for axis, step in exchanges:
         got = swap(held, axis, step)
         if held.shape[0] < devices // 2:
             held = jnp.concatenate([held, got], axis=0)
@@ -394,30 +402,36 @@
         (me,), (held, got, gain),
     )
 
-    both = call(
+    hidden_near, pre_near = call(
         hidden_kernel,
-        shape((2, rows, units), kept),
+        [shape((1, rows, units), kept)] * 2,
         (), (normed, grad_all, turned),
         [pltpu.VMEM((features, units), kept)] * 2,
     )
 
-    near = both[None]
-    for step in dp_steps:
-        far = swap(near, "dp", step)
-        if near.shape[0] < replicas // 2:
-            near = jnp.concatenate([near, far], axis=0)
-
-    grads = weight_grads(me, near, 0, dp_steps, normed, grad_all, width, ())
+    hidden_steps, pre_steps = dp_steps, dp_steps[-1:] + dp_steps[:-1]
+    for hidden_step, pre_step in zip(hidden_steps, pre_steps):
+        hidden_far = swap(hidden_near, "dp", hidden_step)
+        pre_far = swap(pre_near, "dp", pre_step)
+        if hidden_near.shape[0] < replicas // 2:
+            hidden_near = jnp.concatenate([hidden_near, hidden_far], axis=0)
+            pre_near = jnp.concatenate([pre_near, pre_far], axis=0)
+
+    grads = weight_grads(
+        me, hidden_near, pre_near, 0,
+        hidden_steps, pre_steps, normed, grad_all, width, (),
+    )
     tail = call(
-        functools.partial(share_kernel, sections, capacity, dp_steps),
+        functools.partial(share_kernel, sections, capacity, hidden_steps, pre_steps),
         shape((devices, 2 * slots, part), kept),
-        (me,), (near, far, expand_weight, project_turned),
+        (me,), (hidden_near, hidden_far, pre_near, pre_far, expand_weight, project_turned),
     )
     tail = lax.all_to_all(
         tail, ("dp", "section"), split_axis=0, concat_axis=0, tiled=True
     )
     expand_grad, project_grad = weight_grads(
-        me, far, replicas // 2, dp_steps, normed, grad_all, width, grads
+        me, hidden_far, pre_far, replicas // 2,
+        hidden_steps, pre_steps, normed, grad_all, width, grads,
     )
     embedded, grad_rows = call(
         functools.partial(finish_kernel, sections, capacity),

time: 155 us -> 140 us (0.903)
  waiting for transfers between devices: 103 us -> 85.9 us
  starting transfers between devices: 24 us -> 29.7 us
  local copies, waits for them, and re-layouts: 7.93 us -> 4.6 us
    ppermute x8 -> x11, waiting for transfers between devices: 103 us -> 85.9 us  [swap(): return lax.ppermute(array, axis, [(i, i ^ step) for i in range(size)])]
    ppermute x8 -> x11, starting transfers between devices: 11.6 us -> 17.1 us  [swap(): return lax.ppermute(array, axis, [(i, i ^ step) for i in range(size)])]
    unnamed x30 -> x35, local copies, waits for them, and re-layouts: 7.89 us -> 4.52 us
  transfers between devices with their start and end apart: 10 -> 13, of which waited for: 8 -> 11; matrix products, arithmetic and copies ran while one was open for 0% -> 0% of each run, Pallas kernels for 8% -> 9%
where the time goes in v3:
time: 140 us; the launch traced here: 139 us
  waiting for transfers between devices  85.9 us (61%)
  starting transfers between devices  29.7 us (21%)
  Pallas kernels  18.1 us (13%)
  local copies, waits for them, and re-layouts  4.6 us (3%)
    ppermute x11, waiting for transfers between devices, swap(): return lax.ppermute(array, axis, [(i, i ^ step) for i in range(size)])  85.9 us
    ppermute x11, starting transfers between devices, swap(): return lax.ppermute(array, axis, [(i, i ^ step) for i in range(size)])  17.1 us
    pallas_call x2, Pallas kernels, weight_grads(): pl.pallas_call(weight_grad_kernel, grid_spec=pltpu.PrefetchScalarGridSpec...  9.69 us
    pallas_call x6, Pallas kernels, call(): pl.pallas_call(kernel, out_shape=out_shape, in_specs=[SMEM_SPEC] * len(sm...  8.38 us
    all_to_all x1, starting transfers between devices, move_rows_plan(): lax.all_to_all(stacked, 'dp', split_axis=0, concat_axis=0, tiled=True)  7.28 us
    all_to_all x1, starting transfers between devices, move_rows_plan(): lax.all_to_all(tail, ('dp', 'section'), split_axis=0, concat_axis=0, tile...  5.31 us
    unnamed x35, local copies, waits for them, and re-layouts  4.52 us
  transfers between devices with their start and end apart: 13, of which 11 were waited for; matrix products, arithmetic and copies ran while one was open for 0% of the time, Pallas kernels for 9%

profile of v3, /device:TPU:0, one launch (start us, length us, event | category | flops | bytes accessed | tf_op | source)
XLA Modules:
  0.0 139.3 jit_solution(17145181698917245859)
XLA Ops:
  0.7 0.0 copy-start
  0.7 1.1 copy-done
  1.8 1.1 copy-done.2
  3.0 1.3 shard_map.113
  4.2 7.3 %all-to-all-start = ((bf16[8,2,200,256]{3,2,1,0:T(8,128)(2,1)}), bf16[8,2,200,256]{3,2,1,0:T(8,128)(2,1)S(1)}, u32[]{:S(2)}, u32[]{:S(2)}) async-start(bf16[8,2,200,256]{3,2,1,0:T(8,128)(2,1)} %shard_map.113), calls=%async_computation | async-start | bytes 3276800 | tf_op jit(solution)/shard_map/all_to_all | solution.py:387
  11.5 0.1 pad_add_fusion.me_ref
  11.6 0.7 shard_map.111
  12.3 3.0 %collective-permute-start = (bf16[1,16,1600]{2,1,0:T(8,128)(2,1)S(1)}, bf16[1,16,1600]{2,1,0:T(8,128)(2,1)S(1)}, u32[]{:S(2)}, u32[]{:S(2)}) collective-permute-start(bf16[1,16,1600]{2,1,0:T(8,128)(2,1)S(1)} %shard_map.111), channel_id=1, source_target_pairs={{0,16},{4,20},{8,24},{12,28},{16,0},{20,4},{24,8},{28,12},{1,17},{... | collective-permute-start | bytes 153608 | tf_op jit(solution)/shard_map/ppermute | solution.py:113
  15.3 36.9 %collective-permute-done = bf16[1,16,1600]{2,1,0:T(8,128)(2,1)S(1)} collective-permute-done((bf16[1,16,1600]{2,1,0:T(8,128)(2,1)S(1)}, bf16[1,16,1600]{2,1,0:T(8,128)(2,1)S(1)}, u32[]{:S(2)}, u32[]{:S(2)}) %collective-permute-start) | collective-permute-done | bytes 51232 | tf_op jit(solution)/shard_map/ppermute | solution.py:113
  52.2 0.1 collective-permute-start.1
  52.3 4.7 %collective-permute-done.1 = bf16[2,16,1600]{2,1,0:T(8,128)(2,1)S(1)} collective-permute-done((bf16[2,16,1600]{2,1,0:T(8,128)(2,1)S(1)}, bf16[2,16,1600]{2,1,0:T(8,128)(2,1)S(1)}, u32[]{:S(2)}, u32[]{:S(2)}) %collective-permute-start.1) | collective-permute-done | bytes 102432 | tf_op jit(solution)/shard_map/ppermute | solution.py:113
  57.0 1.5 %collective-permute-start.2 = (bf16[4,16,1600]{2,1,0:T(8,128)(2,1)S(1)}, bf16[4,16,1600]{2,1,0:T(8,128)(2,1)S(1)}, u32[]{:S(2)}, u32[]{:S(2)}) collective-permute-start(bf16[4,16,1600]{2,1,0:T(8,128)(2,1)S(1)} %pad_maximum_fusion.3), channel_id=1, source_target_pairs={{0,4},{4,0},{8,12},{12,8},{16,20},{20,16},{24,28},{28,24},{1,5},{5... | collective-permute-start | bytes 614408 | tf_op jit(solution)/shard_map/ppermute | solution.py:113
  58.6 4.4 %collective-permute-done.2 = bf16[4,16,1600]{2,1,0:T(8,128)(2,1)S(1)} collective-permute-done((bf16[4,16,1600]{2,1,0:T(8,128)(2,1)S(1)}, bf16[4,16,1600]{2,1,0:T(8,128)(2,1)S(1)}, u32[]{:S(2)}, u32[]{:S(2)}) %collective-permute-start.2) | collective-permute-done | bytes 204832 | tf_op jit(solution)/shard_map/ppermute | solution.py:113
  63.0 0.1 pad_maximum_fusion
  63.0 1.6 %collective-permute-start.3 = (bf16[8,16,1600]{2,1,0:T(8,128)(2,1)S(1)}, bf16[8,16,1600]{2,1,0:T(8,128)(2,1)S(1)}, u32[]{:S(2)}, u32[]{:S(2)}) collective-permute-start(bf16[8,16,1600]{2,1,0:T(8,128)(2,1)S(1)} %pad_maximum_fusion), channel_id=1, source_target_pairs={{0,2},{1,3},{2,0},{3,1},{4,6},{5,7},{6,4},{7,5},{8,10},{9,11},{10,... | collective-permute-start | bytes 1228808 | tf_op jit(solution)/shard_map/ppermute | solution.py:113
  64.7 6.7 %collective-permute-done.3 = bf16[8,16,1600]{2,1,0:T(8,128)(2,1)S(1)} collective-permute-done((bf16[8,16,1600]{2,1,0:T(8,128)(2,1)S(1)}, bf16[8,16,1600]{2,1,0:T(8,128)(2,1)S(1)}, u32[]{:S(2)}, u32[]{:S(2)}) %collective-permute-start.3) | collective-permute-done | bytes 409632 | tf_op jit(solution)/shard_map/ppermute | solution.py:113
  71.4 0.1 collective-permute-start.4
  71.5 2.3 %collective-permute-done.4.far_ref = bf16[16,16,1600]{2,1,0:T(8,128)(2,1)S(1)} collective-permute-done((bf16[16,16,1600]{2,1,0:T(8,128)(2,1)S(1)}, bf16[16,16,1600]{2,1,0:T(8,128)(2,1)S(1)}, u32[]{:S(2)}, u32[]{:S(2)}) %collective-permute-start.4) | collective-permute-done | bytes 819232 | tf_op jit(solution)/shard_map/ppermute | solution.py:113
  73.8 2.0 %shard_map.112 = (bf16[256,1600]{1,0:T(8,128)(2,1)S(1)}, bf16[256,1600]{1,0:T(8,128)(2,1)S(1)}, f32[16,1600]{1,0:T(8,128)S(1)}) custom-call(s32[2]{0:T(128)S(1)} %pad_add_fusion.me_ref, bf16[16,16,1600]{2,1,0:T(8,128)(2,1)S(1)} %constant_dynamic-update-slice_fusion.near_ref, bf16[16,16,1600]{2,1,0:T(8,128)(2,1)S(1)} %collective-permute-done.4.far_ref, ...), custom_call_target="tpu_custom_call" | custom-call | tf_op jit(solution)/shard_map/pallas_call | solution.py:354
  75.9 0.0 all-to-all-done.turned_ref
  75.9 0.0 copy-start.3
  75.9 0.8 shard_map.114
  76.7 1.8 %collective-permute-start.8 = (bf16[1,256,256]{2,1,0:T(8,128)(2,1)S(1)}, bf16[1,256,256]{2,1,0:T(8,128)(2,1)S(1)}, u32[]{:S(2)}, u32[]{:S(2)}) collective-permute-start(bf16[1,256,256]{2,1,0:T(8,128)(2,1)S(1)} %get-tuple-element.18), channel_id=1, source_target_pairs={{0,4},{4,0},{8,12},{12,8},{16,20},{20,16},{24,28},{28,24},{1,5},{5... | collective-permute-start | bytes 393224 | tf_op jit(solution)/shard_map/ppermute | solution.py:113
  78.5 3.0 %collective-permute-start.5 = (bf16[1,256,256]{2,1,0:T(8,128)(2,1)S(1)}, bf16[1,256,256]{2,1,0:T(8,128)(2,1)S(1)}, u32[]{:S(2)}, u32[]{:S(2)}) collective-permute-start(bf16[1,256,256]{2,1,0:T(8,128)(2,1)S(1)} %get-tuple-element.17), channel_id=1, source_target_pairs={{0,16},{4,20},{8,24},{12,28},{16,0},{20,4},{24,8},{28,12},{1,17},{... | collective-permute-start | bytes 393224 | tf_op jit(solution)/shard_map/ppermute | solution.py:113
  81.5 0.8 collective-permute-done.8
  82.3 4.1 %collective-permute-start.9 = (bf16[2,256,256]{2,1,0:T(8,128)(2,1)S(1)}, bf16[2,256,256]{2,1,0:T(8,128)(2,1)S(1)}, u32[]{:S(2)}, u32[]{:S(2)}) collective-permute-start(bf16[2,256,256]{2,1,0:T(8,128)(2,1)S(1)} %pad_maximum_fusion.2), channel_id=1, source_target_pairs={{0,16},{4,20},{8,24},{12,28},{16,0},{20,4},{24,8},{28,12},{1,17},{... | collective-permute-start | bytes 786440 | tf_op jit(solution)/shard_map/ppermute | solution.py:113
  86.4 7.8 %collective-permute-done.5 = bf16[1,256,256]{2,1,0:T(8,128)(2,1)S(1)} collective-permute-done((bf16[1,256,256]{2,1,0:T(8,128)(2,1)S(1)}, bf16[1,256,256]{2,1,0:T(8,128)(2,1)S(1)}, u32[]{:S(2)}, u32[]{:S(2)}) %collective-permute-start.5) | collective-permute-done | bytes 131104 | tf_op jit(solution)/shard_map/ppermute | solution.py:113
  94.1 0.2 collective-permute-start.6
  94.3 4.8 %collective-permute-done.9 = bf16[2,256,256]{2,1,0:T(8,128)(2,1)S(1)} collective-permute-done((bf16[2,256,256]{2,1,0:T(8,128)(2,1)S(1)}, bf16[2,256,256]{2,1,0:T(8,128)(2,1)S(1)}, u32[]{:S(2)}, u32[]{:S(2)}) %collective-permute-start.9) | collective-permute-done | bytes 262176 | tf_op jit(solution)/shard_map/ppermute | solution.py:113
  99.1 0.0 copy-start.4
  99.2 0.4 collective-permute-start.10
  99.6 5.1 %collective-permute-done.6 = bf16[2,256,256]{2,1,0:T(8,128)(2,1)S(1)} collective-permute-done((bf16[2,256,256]{2,1,0:T(8,128)(2,1)S(1)}, bf16[2,256,256]{2,1,0:T(8,128)(2,1)S(1)}, u32[]{:S(2)}, u32[]{:S(2)}) %collective-permute-start.6) | collective-permute-done | bytes 262176 | tf_op jit(solution)/shard_map/ppermute | solution.py:113
  104.8 0.0 copy-start.6
  104.8 1.4 collective-permute-start.7
  106.1 9.8 %collective-permute-done.10.pre_far_ref.pre_ref = bf16[4,256,256]{2,1,0:T(8,128)(2,1)S(1)} collective-permute-done((bf16[4,256,256]{2,1,0:T(8,128)(2,1)S(1)}, bf16[4,256,256]{2,1,0:T(8,128)(2,1)S(1)}, u32[]{:S(2)}, u32[]{:S(2)}) %collective-permute-start.10) | collective-permute-done | bytes 524320 | tf_op jit(solution)/shard_map/ppermute | solution.py:113
  115.9 2.7 %collective-permute-done.7.hidden_far_ref.hidden_ref = bf16[4,256,256]{2,1,0:T(8,128)(2,1)S(1)} collective-permute-done((bf16[4,256,256]{2,1,0:T(8,128)(2,1)S(1)}, bf16[4,256,256]{2,1,0:T(8,128)(2,1)S(1)}, u32[]{:S(2)}, u32[]{:S(2)}) %collective-permute-start.7) | collective-permute-done | bytes 524320 | tf_op jit(solution)/shard_map/ppermute | solution.py:113
  118.6 0.0 copy-done.1
  118.6 2.1 %shard_map.115 = bf16[32,16,200]{2,1,0:T(8,128)(2,1)} custom-call(s32[2]{0:T(128)S(1)} %pad_add_fusion.me_ref, bf16[4,256,256]{2,1,0:T(8,128)(2,1)S(1)} %constant_dynamic-update-slice_fusion.5.hidden_near_ref.hidden_ref, bf16[4,256,256]{2,1,0:T(8,128)(2,1)S(1)} %collective-permute-done.7.hidden_far_ref.hidden_ref, ...), custom_call_target="tpu_custom_call" | custom-call | tf_op jit(solution)/shard_map/pallas_call | solution.py:354
  120.7 0.0 copy-done.6
  120.7 5.3 %all-to-all-start.1 = ((bf16[32,16,200]{2,1,0:T(8,128)(2,1)}), bf16[32,16,200]{2,1,0:T(8,128)(2,1)S(1)}, u32[]{:S(2)}, u32[]{:S(2)}) async-start(bf16[32,16,200]{2,1,0:T(8,128)(2,1)} %shard_map.115), calls=%async_computation.1 | async-start | bytes 524288 | tf_op jit(solution)/shard_map/all_to_all | solution.py:429
  126.1 0.0 copy-start.5
  126.1 1.0 copy-done.5
  127.1 1.0 copy-done.7
  128.1 4.9 %shard_map.117 = (bf16[1600,2048]{1,0:T(8,128)(2,1)}, bf16[1600,2048]{1,0:T(8,128)(2,1)}) custom-call(s32[2]{0:T(128)S(1)} %pad_add_fusion.me_ref, bf16[4,256,256]{2,1,0:T(8,128)(2,1)S(1)} %copy-done.7, bf16[4,256,256]{2,1,0:T(8,128)(2,1)S(1)} %copy-done.5, bf16[256,1600]{1,0:T(8,128)(2,1)S(1)} %get-tuple-element.15.normed_ref, ...), custom_call_target="tpu_custom_call" | custom-call | flops 1677721600 | bytes 8192000 | tf_op jit(solution)/shard_map/pallas_call | solution.py:327
  133.0 4.8 %shard_map.118 = (bf16[1600,2048]{1,0:T(8,128)(2,1)}, bf16[1600,2048]{1,0:T(8,128)(2,1)}) custom-call(s32[2]{0:T(128)S(1)} %pad_add_fusion.me_ref, bf16[4,256,256]{2,1,0:T(8,128)(2,1)S(1)} %collective-permute-done.7.hidden_far_ref.hidden_ref, ...), custom_call_target="tpu_custom_call", output_to_operand_aliasing={{0}: (5, {}), {1}: (6, {})} | custom-call | flops 1677721600 | bytes 8192000 | tf_op jit(solution)/shard_map/pallas_call | solution.py:327
  137.8 0.0 all-to-all-done.1.tail_ref
  137.8 0.0 copy-done.9
  137.8 1.5 %shard_map.116 = (bf16[16,1600]{1,0:T(8,128)(2,1)}, bf16[8,1600]{1,0:T(8,128)(2,1)}) custom-call(s32[2]{0:T(128)S(1)} %pad_add_fusion.me_ref, s32[1,4]{1,0:T(1,128)S(1)} %copy-done.11, s32[1,8]{1,0:T(1,128)S(1)} %copy-done.12, bf16[32,16,200]{2,1,0:T(8,128)(2,1)S(1)} %all-to-all-done.1.tail_ref, f32[16,1600]{1,0:T(8,128)S(1)} %get-tuple-element.19.extra_ref, ...), custom_call_target="tpu_custom_call" | custom-call | tf_op jit(solution)/shard_map/pallas_call | solution.py:354
  (31 shorter events, 0.3 us)
Async XLA Ops:
  0.6 11.0 %copy-start.12 = (s32[1,8]{1,0:T(1,128)S(1)}, s32[1,8]{1,0:T(1,128)}, u32[]{:S(2)}) copy-start(s32[1,8]{1,0:T(1,128)} %place_ref.3) | copy-start | bytes 100
  0.6 11.0 %copy-start.11 = (s32[1,4]{1,0:T(1,128)S(1)}, s32[1,4]{1,0:T(1,128)}, u32[]{:S(2)}) copy-start(s32[1,4]{1,0:T(1,128)} %count_ref.3) | copy-start | bytes 52
  0.7 1.2 copy-start
  1.8 1.1 copy-start.2
  3.0 8.7 %copy-start.8 = (bf16[8,1600]{1,0:T(8,128)(2,1)S(1)}, bf16[8,1600]{1,0:T(8,128)(2,1)}, u32[]{:S(2)}) copy-start(bf16[8,1600]{1,0:T(8,128)(2,1)} %patch_ref.3) | copy-start | bytes 76804
  3.0 8.7 %copy-start.10 = (bf16[16,1600]{1,0:T(8,128)(2,1)S(1)}, bf16[16,1600]{1,0:T(8,128)(2,1)}, u32[]{:S(2)}) copy-start(bf16[16,1600]{1,0:T(8,128)(2,1)} %cotangent_ref.1) | copy-start | bytes 153604
  3.0 68.5 %copy-start.13 = (f32[1600]{0:T(1024)S(1)}, f32[1600]{0:T(1024)}, u32[]{:S(2)}) copy-start(f32[1600]{0:T(1024)} %param.9) | copy-start | bytes 19204
  4.2 71.6 %all-to-all-start = ((bf16[8,2,200,256]{3,2,1,0:T(8,128)(2,1)}), bf16[8,2,200,256]{3,2,1,0:T(8,128)(2,1)S(1)}, u32[]{:S(2)}, u32[]{:S(2)}) async-start(bf16[8,2,200,256]{3,2,1,0:T(8,128)(2,1)} %shard_map.113), calls=%async_computation | async-start | bytes 3276800 | tf_op jit(solution)/shard_map/all_to_all | solution.py:387
  12.3 39.9 %collective-permute-start = (bf16[1,16,1600]{2,1,0:T(8,128)(2,1)S(1)}, bf16[1,16,1600]{2,1,0:T(8,128)(2,1)S(1)}, u32[]{:S(2)}, u32[]{:S(2)}) collective-permute-start(bf16[1,16,1600]{2,1,0:T(8,128)(2,1)S(1)} %shard_map.111), channel_id=1, source_target_pairs={{0,16},{4,20},{8,24},{12,28},{16,0},{20,4},{24,8},{28,12},{1,17},{... | collective-permute-start | bytes 153608 | tf_op jit(solution)/shard_map/ppermute | solution.py:113
  52.2 4.8 %collective-permute-start.1 = (bf16[2,16,1600]{2,1,0:T(8,128)(2,1)S(1)}, bf16[2,16,1600]{2,1,0:T(8,128)(2,1)S(1)}, u32[]{:S(2)}, u32[]{:S(2)}) collective-permute-start(bf16[2,16,1600]{2,1,0:T(8,128)(2,1)S(1)} %pad_maximum_fusion.4), channel_id=1, source_target_pairs={{0,8},{4,12},{8,0},{12,4},{16,24},{20,28},{24,16},{28,20},{1,9},{5... | collective-permute-start | bytes 307208 | tf_op jit(solution)/shard_map/ppermute | solution.py:113
  57.0 5.9 %collective-permute-start.2 = (bf16[4,16,1600]{2,1,0:T(8,128)(2,1)S(1)}, bf16[4,16,1600]{2,1,0:T(8,128)(2,1)S(1)}, u32[]{:S(2)}, u32[]{:S(2)}) collective-permute-start(bf16[4,16,1600]{2,1,0:T(8,128)(2,1)S(1)} %pad_maximum_fusion.3), channel_id=1, source_target_pairs={{0,4},{4,0},{8,12},{12,8},{16,20},{20,16},{24,28},{28,24},{1,5},{5... | collective-permute-start | bytes 614408 | tf_op jit(solution)/shard_map/ppermute | solution.py:113
  63.0 8.3 %collective-permute-start.3 = (bf16[8,16,1600]{2,1,0:T(8,128)(2,1)S(1)}, bf16[8,16,1600]{2,1,0:T(8,128)(2,1)S(1)}, u32[]{:S(2)}, u32[]{:S(2)}) collective-permute-start(bf16[8,16,1600]{2,1,0:T(8,128)(2,1)S(1)} %pad_maximum_fusion), channel_id=1, source_target_pairs={{0,2},{1,3},{2,0},{3,1},{4,6},{5,7},{6,4},{7,5},{8,10},{9,11},{10,... | collective-permute-start | bytes 1228808 | tf_op jit(solution)/shard_map/ppermute | solution.py:113
  71.4 2.4 %collective-permute-start.4 = (bf16[16,16,1600]{2,1,0:T(8,128)(2,1)S(1)}, bf16[16,16,1600]{2,1,0:T(8,128)(2,1)S(1)}, u32[]{:S(2)}, u32[]{:S(2)}) collective-permute-start(bf16[16,16,1600]{2,1,0:T(8,128)(2,1)S(1)} %constant_dynamic-update-slice_fusion.near_ref), channel_id=1, source_target_pairs={{0,1},{1,0},{2,3},{3,2},{4,5},{5,4},{6,7},{7,6},{8,9},{9,8},{10,11... | collective-permute-start | bytes 2457608 | tf_op jit(solution)/shard_map/ppermute | solution.py:113
  75.9 42.7 %copy-start.1 = (bf16[200,2048]{1,0:T(8,128)(2,1)S(1)}, bf16[200,2048]{1,0:T(8,128)(2,1)}, u32[]{:S(2)}) copy-start(bf16[200,2048]{1,0:T(8,128)(2,1)} %expand_ref.3) | copy-start | bytes 2457604
  75.9 42.7 %copy-start.3 = (bf16[2048,200]{0,1:T(8,128)(2,1)S(1)}, bf16[2048,200]{0,1:T(8,128)(2,1)}, u32[]{:S(2)}) copy-start(bf16[2048,200]{0,1:T(8,128)(2,1)} %param.11) | copy-start | bytes 2457604
  76.7 5.6 %collective-permute-start.8 = (bf16[1,256,256]{2,1,0:T(8,128)(2,1)S(1)}, bf16[1,256,256]{2,1,0:T(8,128)(2,1)S(1)}, u32[]{:S(2)}, u32[]{:S(2)}) collective-permute-start(bf16[1,256,256]{2,1,0:T(8,128)(2,1)S(1)} %get-tuple-element.18), channel_id=1, source_target_pairs={{0,4},{4,0},{8,12},{12,8},{16,20},{20,16},{24,28},{28,24},{1,5},{5... | collective-permute-start | bytes 393224 | tf_op jit(solution)/shard_map/ppermute | solution.py:113
  78.5 15.7 %collective-permute-start.5 = (bf16[1,256,256]{2,1,0:T(8,128)(2,1)S(1)}, bf16[1,256,256]{2,1,0:T(8,128)(2,1)S(1)}, u32[]{:S(2)}, u32[]{:S(2)}) collective-permute-start(bf16[1,256,256]{2,1,0:T(8,128)(2,1)S(1)} %get-tuple-element.17), channel_id=1, source_target_pairs={{0,16},{4,20},{8,24},{12,28},{16,0},{20,4},{24,8},{28,12},{1,17},{... | collective-permute-start | bytes 393224 | tf_op jit(solution)/shard_map/ppermute | solution.py:113
  82.3 16.8 %collective-permute-start.9 = (bf16[2,256,256]{2,1,0:T(8,128)(2,1)S(1)}, bf16[2,256,256]{2,1,0:T(8,128)(2,1)S(1)}, u32[]{:S(2)}, u32[]{:S(2)}) collective-permute-start(bf16[2,256,256]{2,1,0:T(8,128)(2,1)S(1)} %pad_maximum_fusion.2), channel_id=1, source_target_pairs={{0,16},{4,20},{8,24},{12,28},{16,0},{20,4},{24,8},{28,12},{1,17},{... | collective-permute-start | bytes 786440 | tf_op jit(solution)/shard_map/ppermute | solution.py:113
  94.1 10.6 %collective-permute-start.6 = (bf16[2,256,256]{2,1,0:T(8,128)(2,1)S(1)}, bf16[2,256,256]{2,1,0:T(8,128)(2,1)S(1)}, u32[]{:S(2)}, u32[]{:S(2)}) collective-permute-start(bf16[2,256,256]{2,1,0:T(8,128)(2,1)S(1)} %pad_maximum_fusion.1), channel_id=1, source_target_pairs={{0,8},{4,12},{8,0},{12,4},{16,24},{20,28},{24,16},{28,20},{1,9},{5... | collective-permute-start | bytes 786440 | tf_op jit(solution)/shard_map/ppermute | solution.py:113
  99.1 19.4 %copy-start.4 = (bf16[4,256,256]{2,1,0:T(8,128)(2,1)}, bf16[4,256,256]{2,1,0:T(8,128)(2,1)S(1)}, u32[]{:S(2)}) copy-start(bf16[4,256,256]{2,1,0:T(8,128)(2,1)S(1)} %constant_dynamic-update-slice_fusion.8.pre_near_ref.pre_ref) | copy-start | bytes 1572868
  99.2 16.7 %collective-permute-start.10 = (bf16[4,256,256]{2,1,0:T(8,128)(2,1)S(1)}, bf16[4,256,256]{2,1,0:T(8,128)(2,1)S(1)}, u32[]{:S(2)}, u32[]{:S(2)}) collective-permute-start(bf16[4,256,256]{2,1,0:T(8,128)(2,1)S(1)} %constant_dynamic-update-slice_fusion.8.pre_near_ref.pre_ref), channel_id=1, source_target_pairs={{0,8},{4,12},{8,0},{12,4},{16,24},{20,28},{24,16},{28,20},{1,9},{5... | collective-permute-start | bytes 1572872 | tf_op jit(solution)/shard_map/ppermute | solution.py:113
  104.8 16.0 %copy-start.6 = (bf16[4,256,256]{2,1,0:T(8,128)(2,1)}, bf16[4,256,256]{2,1,0:T(8,128)(2,1)S(1)}, u32[]{:S(2)}) copy-start(bf16[4,256,256]{2,1,0:T(8,128)(2,1)S(1)} %constant_dynamic-update-slice_fusion.5.hidden_near_ref.hidden_ref) | copy-start | bytes 1572868
  104.8 13.8 %collective-permute-start.7 = (bf16[4,256,256]{2,1,0:T(8,128)(2,1)S(1)}, bf16[4,256,256]{2,1,0:T(8,128)(2,1)S(1)}, u32[]{:S(2)}, u32[]{:S(2)}) collective-permute-start(bf16[4,256,256]{2,1,0:T(8,128)(2,1)S(1)} %constant_dynamic-update-slice_fusion.5.hidden_near_ref.hidden_ref), channel_id=1, source_target_pairs={{0,4},{4,0},{8,12},{12,8},{16,20},{20,16},{24,28},{28,24},{1,5},{5... | collective-permute-start | bytes 1572872 | tf_op jit(solution)/shard_map/ppermute | solution.py:113
  120.7 17.1 %all-to-all-start.1 = ((bf16[32,16,200]{2,1,0:T(8,128)(2,1)}), bf16[32,16,200]{2,1,0:T(8,128)(2,1)S(1)}, u32[]{:S(2)}, u32[]{:S(2)}) async-start(bf16[32,16,200]{2,1,0:T(8,128)(2,1)} %shard_map.115), calls=%async_computation.1 | async-start | bytes 524288 | tf_op jit(solution)/shard_map/all_to_all | solution.py:429
  126.1 1.0 copy-start.5
  127.1 1.0 copy-start.7
  133.0 4.8 %copy-start.9 = (bf16[16,1600]{1,0:T(8,128)(2,1)S(1)}, bf16[16,1600]{1,0:T(8,128)(2,1)}, u32[]{:S(2)}) copy-start(bf16[16,1600]{1,0:T(8,128)(2,1)} %text_ref.1) | copy-start | bytes 153604
